TPU v7x, 128 devices: a whole 4x4x4 slice. The times are simulated.
128 devices in a mesh: ctx: 64 (over z, y, x_hi, core), head: 2 (over x_lo).
Axes of the slice: x: 4 (x_hi: 2, x_lo: 2; x = x_hi * 2 + x_lo), y: 4, z: 4, core: 2. Of those that a mesh axis runs over, the one named last changes fastest.
Arguments:
- key_rows: bfloat16 [65536, 2560], P('ctx', 'head'), may hold values from -6 to 6
- value_rows: bfloat16 [65536, 2560], P('ctx', 'head'), may hold values from -6 to 6
- query_rows: bfloat16 [65536, 2560], P('ctx', 'head'), may hold values from -6 to 6
- learn_rates: float32 [4, 65536], P('head', 'ctx'), may hold values from 5e-05 to 0.0005
- fast_in: bfloat16 [4, 640, 640], P('head'), may hold values from -0.25 to 0.25
- fast_gate: bfloat16 [4, 640, 640], P('head'), may hold values from -0.25 to 0.25
- fast_out: bfloat16 [4, 640, 640], P('head'), may hold values from -0.25 to 0.25
- head_gain: float32 [2560], P('head'), may hold values from 0.1 to 1.9
- out_proj: bfloat16 [2560, 2560], P('head', 'ctx'), may hold values from -0.3125 to 0.3125
Outputs:
- output: bfloat16 [65536, 2560], P('ctx', 'head')
- new_in: bfloat16 [4, 640, 640], P('head')
- new_gate: bfloat16 [4, 640, 640], P('head')
- new_out: bfloat16 [4, 640, 640], P('head')
All inputs are finite; a program needn't handle non-finite values.
Results may differ from a plain program's by a relative error of at most 0.012.
Values may be sent and summed in bfloat16 or wider, within the bound.
A program may use at most 128 MiB of HBM per device.

v0:
```python
import jax
import jax.numpy as jnp
from jax import lax
from jax.sharding import PartitionSpec as P


def renorm(weight, grad):
    wide = weight.astype(jnp.float32)
    moved = wide - grad
    scale = jnp.sqrt(jnp.sum(wide * wide, axis=1, keepdims=True) + 1e-06) / jnp.sqrt(
        jnp.sum(moved * moved, axis=1, keepdims=True) + 1e-06
    )
    return (moved * scale).astype(jnp.bfloat16)


def on_device(
    key_rows, value_rows, query_rows, learn_rates, fast_in, fast_gate, fast_out, head_gain, out_proj
):
    tok_count = key_rows.shape[0]
    local_heads = fast_in.shape[0]
    head_width = fast_in.shape[1]
    keyed = key_rows.reshape(tok_count, local_heads, head_width)
    valued = value_rows.reshape(tok_count, local_heads, head_width)
    queried = query_rows.reshape(tok_count, local_heads, head_width)
    pre_in = jnp.einsum("thd,hdf->thf", keyed, fast_in, preferred_element_type=jnp.float32)
    pre_gate = jnp.einsum("thd,hdf->thf", keyed, fast_gate, preferred_element_type=jnp.float32)
    sig = jax.nn.sigmoid(pre_in)
    act = pre_in * sig
    hidden = (act * pre_gate).astype(jnp.bfloat16)
    rate_cols = learn_rates.T[:, :, None]
    err = (-rate_cols * valued.astype(jnp.float32)).astype(jnp.bfloat16)
    grad_out = jnp.einsum("thf,thd->hfd", hidden, err, preferred_element_type=jnp.float32)
    back = jnp.einsum("thd,hfd->thf", err, fast_out, preferred_element_type=jnp.float32)
    back_in = (back * pre_gate * sig * (1.0 + pre_in * (1.0 - sig))).astype(jnp.bfloat16)
    back_gate = (back * act).astype(jnp.bfloat16)
    grad_in = jnp.einsum("thd,thf->hdf", keyed, back_in, preferred_element_type=jnp.float32)
    grad_gate = jnp.einsum("thd,thf->hdf", keyed, back_gate, preferred_element_type=jnp.float32)
    sum_in, sum_gate, sum_out = lax.psum((grad_in, grad_gate, grad_out), "ctx")
    upd_in = renorm(fast_in, sum_in)
    upd_gate = renorm(fast_gate, sum_gate)
    upd_out = renorm(fast_out, sum_out)
    q_in = jnp.einsum("thd,hdf->thf", queried, upd_in, preferred_element_type=jnp.float32)
    q_gate = jnp.einsum("thd,hdf->thf", queried, upd_gate, preferred_element_type=jnp.float32)
    q_hidden = (jax.nn.silu(q_in) * q_gate).astype(jnp.bfloat16)
    head_out = jnp.einsum("thf,hfd->thd", q_hidden, upd_out, preferred_element_type=jnp.float32)
    inverse = lax.rsqrt(jnp.mean(head_out * head_out, axis=-1, keepdims=True) + 1e-06)
    gains = head_gain.reshape(local_heads, head_width)
    normed = (
        (head_out * inverse * gains)
        .astype(jnp.bfloat16)
        .reshape(tok_count, local_heads * head_width)
    )
    partial_out = jnp.dot(
        normed,
        lax.all_gather(out_proj, "ctx", axis=1, tiled=True),
        preferred_element_type=jnp.float32,
    )
    output = lax.psum_scatter(
        partial_out.astype(jnp.bfloat16), "head", scatter_dimension=1, tiled=True
    )
    return (output, upd_in, upd_gate, upd_out)


def solution(mesh):
    return jax.shard_map(
        on_device,
        mesh=mesh,
        in_specs=(
            P("ctx", "head"),
            P("ctx", "head"),
            P("ctx", "head"),
            P("head", "ctx"),
            P("head", None, None),
            P("head", None, None),
            P("head", None, None),
            P("head"),
            P("head", "ctx"),
        ),
        out_specs=(
            P("ctx", "head"),
            P("head", None, None),
            P("head", None, None),
            P("head", None, None),
        ),
        check_vma=False,
    )
```

profile of v0, /device:TPU:1, one launch (start us, length us, event | category | flops | bytes accessed | tf_op | source)
XLA Modules:
  0.0 886.3 jit_solution(8439314141396544003)
XLA Ops:
  7.2 0.0 all-reduce.3.cloned.1.call-start
  7.2 0.0 copy-start.8
  7.2 0.0 copy-start.11
  7.2 7.1 fusion.27
  14.3 0.0 copy-done.8
  14.3 0.0 copy-done.11
  14.3 0.0 copy-start.7
  14.3 4.8 fusion.29
  19.1 0.0 copy-done.7
  19.1 0.4 convert_element_type.60
  19.5 0.3 copy-done.9
  19.8 0.7 copy-done
  20.6 2.3 fusion.50
  22.9 8.3 fusion.20
  31.2 9.0 %fusion.34 = f32[2,640,640]{1,2,0:T(8,128)} fusion(f32[2,1024,640]{1,2,0:T(8,128)S(1)} %fusion.50, f32[2,640,1024]{2,1,0:T(8,128)} %fusion.27, f32[2,640,1024]{2,1,0:T(8,128)} %fusion.29, bf16[128,2,8,640]{3,2,1,0:T(8,128)(2,1)S(1)} %bitcast.131), kind=kOutput, calls=%fused_computation.55 | convolution fusion | flops 1690828800 | bytes 21626880 | tf_op jit(solution)/shard_map/thd,thf->hdf/dot_general | solution.py:36
  40.2 6.6 fusion.39
  46.8 0.0 all-reduce.3.cloned.1.call-update
  46.8 0.0 all-gather.2.cloned.1.call-start
  46.9 0.7 all-gather.2.cloned.1.call-update
  47.6 0.0 reduce-scatter.2.cloned.1.call-start
  47.6 2.2 copy.18
  49.8 2.8 copy.22
  52.6 0.0 copy-start.10
  52.6 4.4 copy.34
  57.0 0.0 copy-done.10
  57.0 662.8 %all-reduce.3.cloned.1.call-done = (f32[2,640,640]{2,1,0:T(8,128)}, f32[2,640,640]{1,2,0:T(8,128)}, f32[2,640,640]{1,2,0:T(8,128)}) async-done(((f32[2,640,640]{2,1,0:T(8,128)}, f32[2,640,640]{1,2,0:T(8,128)}, f32[2,640,640]{1,2,0:T(8,128)}), (f32[2,640,640]{2,1,0:T(8,128)}, f32[2,640,640]{1,2,0:T(8,128)}, f32[2,640,640]{1,2,0:T(8,128)})) %all-reduce.3.cloned.1.call-update) | async-done | bytes 9830416 | tf_op jit(solution)/shard_map/psum | solution.py:38
  719.9 2.7 fusion.17
  722.6 0.0 copy-done.1
  722.6 0.6 copy-done.2
  723.3 3.5 fusion.18
  726.8 0.0 copy-done.4
  726.8 0.0 copy-start.3
  726.8 1.7 multiply_convert_fusion.2
  728.5 0.8 copy-done.3
  729.4 0.5 multiply_convert_fusion.1
  729.8 0.0 copy-start.6
  729.9 1.6 multiply_convert_fusion
  731.5 0.7 copy-done.6
  732.2 4.6 fusion.57
  736.8 0.0 copy-done.5
  736.8 10.7 %fusion.1 = (f32[1024,2]{0,1:T(2,128)S(1)}, f32[2,640,1024]{2,1,0:T(8,128)}) fusion(bf16[2,640,640]{2,1,0:T(8,128)(2,1)} %multiply_convert_fusion.2, f32[2,640,1024]{2,1,0:T(8,128)} %fusion.57, bf16[2,640,640]{1,2,0:T(8,128)(2,1)S(1)} %copy-done.5, bf16[1024,2,640]{0,2,1:T(8,128)(2,1)} %bitcast.126), kind=kOutput, calls=%fused_computation.5 | convolution fusion | flops 3365926912 | bytes 16392192 | tf_op jit(solution)/shard_map/thf,hfd->thd/dot_general | solution.py:45
  747.4 4.5 fusion.3
  751.9 49.1 %all-gather.2.cloned.1.call-done = bf16[1280,2560]{0,1:T(8,128)(2,1)} async-done(((bf16[1280,40]{0,1:T(8,128)(2,1)}), bf16[1280,2560]{0,1:T(8,128)(2,1)}) %all-gather.2.cloned.1.call-update) | async-done | bytes 6553616 | tf_op jit(solution)/shard_map/all_gather | solution.py:55
  801.0 12.0 %convolution_convert_fusion = bf16[1024,2560]{1,0:T(8,128)(2,1)} fusion(bf16[1024,1280]{0,1:T(8,128)(2,1)} %bitcast.128, bf16[1280,2560]{0,1:T(8,128)(2,1)} %all-gather.2.cloned.1.call-done), kind=kOutput, calls=%fused_computation | convolution fusion | flops 6713507840 | bytes 14417920 | tf_op jit(solution)/shard_map/dot_general | solution.py:53
  813.0 0.0 reduce-scatter.2.cloned.1.call-update
  813.0 2.2 copy.26
  815.2 2.2 copy.27
  817.4 62.3 %reduce-scatter.2.cloned.1.call-done = bf16[1024,1280]{1,0:T(8,128)(2,1)} async-done(((bf16[1024,2560]{1,0:T(8,128)(2,1)}), bf16[1024,1280]{1,0:T(8,128)(2,1)}) %reduce-scatter.2.cloned.1.call-update) | async-done | bytes 2621456 | tf_op jit(solution)/shard_map/reduce_scatter | solution.py:58
  (12 shorter events, 0.1 us)
Async XLA Ops:
  7.2 712.7 %all-reduce.3.cloned.1.call-start = ((), (), s32[]{:S(2)}) async-start(), calls=%async_computation.3 | async-start | bytes 19660800 | tf_op jit(solution)/shard_map/psum | solution.py:38
  7.2 7.1 copy-start.8
  7.2 7.1 copy-start.11
  14.3 4.8 copy-start.7
  19.1 0.7 copy-start.9
  19.1 1.4 copy-start
  46.8 754.2 %all-gather.2.cloned.1.call-start = ((), (), s32[]{:S(2)}) async-start(), calls=%async_computation.1 | async-start | bytes 6656000 | tf_op jit(solution)/shard_map/all_gather | solution.py:55
  47.6 832.2 %reduce-scatter.2.cloned.1.call-start = ((), (), s32[]{:S(2)}) async-start(), calls=%async_computation.2 | async-start | bytes 7864320 | tf_op jit(solution)/shard_map/reduce_scatter | solution.py:58
  52.6 4.4 copy-start.10
  719.9 2.8 copy-start.1
  719.9 3.4 copy-start.2
  723.3 3.6 copy-start.4
  726.8 2.5 copy-start.3
  729.8 2.3 copy-start.6
  732.2 4.6 copy-start.5
Sparse Core Ops, SparseCore 0:
  46.9 672.8 all-reduce.2
  722.9 78.0 all-gather.1
  813.1 66.5 reduce-scatter.1
where the time goes:
time: 887 us; the launch traced here: 886 us
  waiting for transfers between devices  775 us (87%)
  matrix products  65.3 us (7%)
  local copies, waits for them, and re-layouts  17 us (2%)
  other arithmetic  15 us (2%)
  between operations  13.9 us (2%)
    psum x1, waiting for transfers between devices, on_device(): sum_in, sum_gate, sum_out = lax.psum((grad_in, grad_gate, grad_out), 'ctx')  663 us
    reduce_scatter x1, waiting for transfers between devices, on_device(): lax.psum_scatter(partial_out.astype(jnp.bfloat16), 'head', scatter_dimens...  62.3 us
    all_gather x1, waiting for transfers between devices, on_device(): lax.all_gather(out_proj, 'ctx', axis=1, tiled=True)  49.1 us
  transfers between devices with their start and end apart: 3, of which 3 were waited for; matrix products, arithmetic and copies ran while one was open for 5% of the time, Pallas kernels for 0%

commit v1 on v0

v1 whole, which is shorter than its diff:
```python
import functools

import jax
import jax.numpy as jnp
from jax import lax
from jax.experimental import pallas as pl
from jax.experimental.pallas import tpu as pltpu
from jax.sharding import PartitionSpec as P

MESH = pl.DeviceIdType.MESH
W = 640
R = 2048
PART = R // 4
F32 = jnp.float32
BF16 = jnp.bfloat16
VMEM_LIMIT = 60 * 1024 * 1024


def dot(a, b, dims):
    return lax.dot_general(a, b, ((dims[0], dims[1]), ((), ())), preferred_element_type=F32)


def grad_kernel(
    meta, k_ref, v_ref, lr_ref, wi_ref, wg_ref, wo_ref, gain_ref,
    send_ref, keep_ref, aux_ref, wcat, gcat, gout,
):
    i, t = pl.program_id(0), pl.program_id(1)

    @pl.when(t == 0)
    def _():
        wcat[:, :W] = wi_ref[...]
        wcat[:, W:] = wg_ref[...]
        gcat[...] = jnp.zeros_like(gcat)
        gout[...] = jnp.zeros_like(gout)
        aux_ref[...] = jnp.zeros_like(aux_ref)
        for n, ref in enumerate((wi_ref, wg_ref, wo_ref)):
            wide = ref[...].astype(F32)
            aux_ref[n : n + 1, :] = jnp.sum(wide * wide, axis=0, keepdims=True)
        aux_ref[3:4, :] = gain_ref[...]

    k = k_ref[...]
    pre = dot(k, wcat[...], ((1,), (0,)))
    pre_in, pre_gate = pre[:, :W], pre[:, W:]
    sig = jax.nn.sigmoid(pre_in)
    act = pre_in * sig
    hidden = (act * pre_gate).astype(BF16)
    err = (lr_ref[...] * v_ref[...].astype(F32)).astype(BF16)
    gout[...] += dot(hidden, err, ((0,), (0,)))
    back = dot(err, wo_ref[...], ((1,), (1,)))
    back_in = (back * pre_gate * sig * (1.0 + pre_in * (1.0 - sig))).astype(BF16)
    back_gate = (back * act).astype(BF16)
    gcat[...] += dot(k, jnp.concatenate([back_in, back_gate], axis=1), ((0,), (0,)))

    last = t == pl.num_programs(1) - 1

    @pl.when(last & (i == 0))
    def _():
        send_ref[:W, :] = gcat[:, :W].astype(BF16)
        send_ref[W : 2 * W, :] = gcat[:, W:].astype(BF16)
        send_ref[2 * W : 3 * W, :] = gout[...].astype(BF16)
        send_ref[3 * W :, :] = jnp.zeros((R - 3 * W, W), BF16)

    @pl.when(last & (i == 1))
    def _():
        keep_ref[:W, :] = gcat[:, :W]
        keep_ref[W : 2 * W, :] = gcat[:, W:]
        keep_ref[2 * W : 3 * W, :] = gout[...]
        keep_ref[3 * W :, :] = jnp.zeros((R - 3 * W, W), F32)
        for part in range(4):
            row = meta[1 + part]
            for n, ref in enumerate((wi_ref, wg_ref, wo_ref)):

                @pl.when((row >= n * W) & (row < (n + 1) * W))
                def _():
                    src = pl.ds(pl.multiple_of(row - n * W, 16), 16)
                    dst = pl.ds(pl.multiple_of(row, 16), 16)
                    keep_ref[dst, :] += ref[src, :].astype(F32)


def gradients(meta, k, v, lr, wi, wg, wo, gain, tm=256):
    tok = k.shape[0]

    def head(i, m):
        return (1 - m[0]) + i * (2 * m[0] - 1)

    tile = pl.BlockSpec((tm, W), lambda i, t, m: (t, head(i, m)))
    weight = pl.BlockSpec((None, W, W), lambda i, t, m: (head(i, m), 0, 0))
    return pl.pallas_call(
        grad_kernel,
        grid_spec=pltpu.PrefetchScalarGridSpec(
            num_scalar_prefetch=1,
            grid=(2, tok // tm),
            in_specs=[
                tile,
                tile,
                pl.BlockSpec((None, tm, 1), lambda i, t, m: (head(i, m), t, 0)),
                weight,
                weight,
                weight,
                pl.BlockSpec((None, 1, W), lambda i, t, m: (head(i, m), 0, 0)),
            ],
            out_specs=[
                pl.BlockSpec((R, W), lambda i, t, m: (0, 0)),
                pl.BlockSpec((R, W), lambda i, t, m: (0, 0)),
                pl.BlockSpec((None, 8, W), lambda i, t, m: (head(i, m), 0, 0)),
            ],
            scratch_shapes=[
                pltpu.VMEM((W, 2 * W), BF16),
                pltpu.VMEM((W, 2 * W), F32),
                pltpu.VMEM((W, W), F32),
            ],
        ),
        out_shape=[
            jax.ShapeDtypeStruct((R, W), BF16),
            jax.ShapeDtypeStruct((R, W), F32),
            jax.ShapeDtypeStruct((2, 8, W), F32),
        ],
        compiler_params=pltpu.CompilerParams(vmem_limit_bytes=VMEM_LIMIT),
        cost_estimate=pl.CostEstimate(
            flops=24 * tok * W * W, bytes_accessed=20_000_000, transcendentals=2 * tok * W
        ),
        name="gradients",
    )(meta, k, v, lr, wi, wg, wo, gain)


def position():
    ctx, x_lo = lax.axis_index("ctx"), lax.axis_index("head")
    core, x_hi = ctx % 2, (ctx // 2) % 2
    y, z = (ctx // 4) % 4, ctx // 16
    return z, y, x_hi, core, x_lo


def ctx_of(z, y, x_hi, core):
    return ((z * 4 + y) * 2 + x_hi) * 2 + core


def bits_of(z, y):
    return ((y + 1) // 2) % 2, ((z + 1) // 2) % 2, y // 2, z // 2


def flip(r):
    return r + 1 - 2 * (r % 2)


def final_rows():
    z, y, x_hi, _, _ = position()
    bits = bits_of(z, y)
    rows = []
    for part in range(4):
        base = part * PART
        for step in range(4):
            base = base + bits[(part + step) % 4] * (PART >> (step + 1))
        rows.append(base + x_hi * 16)
    return rows


def reduce_kernel(
    send_ref, keep_ref, aux_ref, u_ref, auxo_ref,
    acc, core_buf, s0, s1, s2, s3, s4, r0, r1, r2, r3, r4, shard,
    s_sem, r_sem, sx_sem, rx_sem, g_ssem, g_rsem, l_sem, x_ssem, x_rsem,
):
    z, y, x_hi, core, x_lo = position()
    bits = bits_of(z, y)
    peers = (
        (ctx_of(z, flip(y), x_hi, core), x_lo),
        (ctx_of(flip(z), y, x_hi, core), x_lo),
        (ctx_of(z, 3 - y, x_hi, core), x_lo),
        (ctx_of(3 - z, y, x_hi, core), x_lo),
    )
    far = (ctx_of(z, y, 1 - x_hi, core), x_lo)
    mate = (ctx_of(z, y, x_hi, 1 - core), x_lo)
    side = (ctx_of(z, y, x_hi, core), 1 - x_lo)
    cross = (ctx_of(z, y, 1 - x_hi, core), 1 - x_lo)

    barrier = pltpu.get_barrier_semaphore()
    for dev in (*peers, far, mate, side, cross):
        pl.semaphore_signal(barrier, inc=1, device_id=dev, device_id_type=MESH)
    pl.semaphore_wait(barrier, 8)

    def remote(src, dst, ssem, rsem, dev):
        return pltpu.make_async_remote_copy(
            src_ref=src, dst_ref=dst, send_sem=ssem, recv_sem=rsem,
            device_id=dev, device_id_type=MESH,
        )

    started = []
    first = remote(send_ref, core_buf, sx_sem.at[0], rx_sem.at[0], mate)
    first.start()
    auxc = remote(aux_ref, auxo_ref, sx_sem.at[1], rx_sem.at[1], side)
    auxc.start()
    first.wait()

    sbuf, rbuf = (s0, s1, s2, s3, s4), (r0, r1, r2, r3, r4)
    base = [p * PART for p in range(4)]
    copies = [[None] * 4 for _ in range(5)]
    CH = 16

    def rows_loop(count, fn):
        def body(n, carry):
            fn(pl.multiple_of(n * CH, CH))
            return carry

        lax.fori_loop(0, count // CH, body, 0)

    for step in range(5):
        half = (PART >> (step + 1)) if step < 4 else 16
        kept_at = [None] * 4
        for p in range(4):
            d = (p + step) % 4
            bit = bits[d] if step < 4 else x_hi
            out_at = base[p] + (1 - bit) * half
            kept_at[p] = base[p] + bit * half
            if step > 0:
                copies[step - 1][p].wait_recv()
            into = sbuf[step].at[p]
            if step == 0:

                def emit(o, out_at=out_at, into=into):
                    at = pl.ds(pl.multiple_of(out_at + o, CH), CH)
                    into[pl.ds(o, CH), :] = (
                        keep_ref[at, :] + core_buf[at, :].astype(F32)
                    ).astype(BF16)
            else:
                prev = rbuf[step - 1].at[p]
                rel = (1 - bit) * half

                def emit(o, out_at=out_at, into=into, prev=prev, rel=rel):
                    at = pl.ds(pl.multiple_of(out_at + o, CH), CH)
                    got = pl.ds(pl.multiple_of(rel + o, CH), CH)
                    into[pl.ds(o, CH), :] = (acc[at, :] + prev[got, :].astype(F32)).astype(BF16)

            rows_loop(half, emit)
            copies[step][p] = remote(
                sbuf[step].at[p], rbuf[step].at[p], s_sem.at[step, p], r_sem.at[step, p],
                peers[d] if step < 4 else far,
            )
            copies[step][p].start()
        for p in range(4):
            if step == 0:

                def hold(o, at0=kept_at[p]):
                    at = pl.ds(pl.multiple_of(at0 + o, CH), CH)
                    acc[at, :] = keep_ref[at, :] + core_buf[at, :].astype(F32)
            else:
                prev = rbuf[step - 1].at[p]
                bit = bits[(p + step) % 4] if step < 4 else x_hi

                def hold(o, at0=kept_at[p], prev=prev, rel=bit * half):
                    at = pl.ds(pl.multiple_of(at0 + o, CH), CH)
                    got = pl.ds(pl.multiple_of(rel + o, CH), CH)
                    acc[at, :] = acc[at, :] + prev[got, :].astype(F32)

            rows_loop(half, hold)
            base[p] = kept_at[p]

    own = 2 * x_lo + core
    locals_, gathers = [], [[None] * 4 for _ in range(5)]
    for p in range(4):
        copies[4][p].wait_recv()
        at = pl.ds(pl.multiple_of(base[p], 16), 16)
        shard[p, :, :] = (acc[at, :] + r4[p, :, :].astype(F32)).astype(BF16)
        dst = u_ref.at[own, at]
        gathers[4][p] = remote(shard.at[p], dst, g_ssem.at[4, p], g_rsem.at[4, p], far)
        gathers[4][p].start()
        local = pltpu.make_async_copy(shard.at[p], dst, l_sem.at[p])
        local.start()
        locals_.append(local)
        base[p] = base[p] - x_hi * 16
    for p in range(4):
        locals_[p].wait()
    size = 32
    for step in range(3, -1, -1):
        for p in range(4):
            d = (p + step) % 4
            gathers[step + 1][p].wait_recv()
            block = u_ref.at[own, pl.ds(pl.multiple_of(base[p], 32), size)]
            gathers[step][p] = remote(block, block, g_ssem.at[step, p], g_rsem.at[step, p], peers[d])
            gathers[step][p].start()
            base[p] = base[p] - bits[d] * size
        size *= 2
    for p in range(4):
        gathers[0][p].wait_recv()

    HALF = 3 * W // 2
    whole = u_ref.at[own, pl.ds(0, 3 * W)]
    to_mate = remote(whole, whole, x_ssem.at[0], x_rsem.at[0], mate)
    low, high = u_ref.at[own, pl.ds(0, HALF)], u_ref.at[own, pl.ds(HALF, HALF)]
    to_side = remote(low, low, x_ssem.at[1], x_rsem.at[1], side)
    to_cross = remote(high, high, x_ssem.at[2], x_rsem.at[2], cross)
    to_side.start()
    to_cross.start()
    to_mate.start()
    other = 2 * (1 - x_lo) + core
    to_side.wait_recv()
    low = u_ref.at[other, pl.ds(0, HALF)]
    fwd_low = remote(low, low, x_ssem.at[3], x_rsem.at[3], mate)
    fwd_low.start()
    to_cross.wait_recv()
    high = u_ref.at[other, pl.ds(HALF, HALF)]
    fwd_high = remote(high, high, x_ssem.at[4], x_rsem.at[4], mate)
    fwd_high.start()
    for copy in (to_mate, fwd_low, fwd_high):
        copy.wait_recv()
    auxc.wait()
    for copy in (to_mate, to_side, to_cross, fwd_low, fwd_high):
        copy.wait_send()
    for step in range(5):
        for p in range(4):
            copies[step][p].wait_send()
            gathers[step][p].wait_send()


def reduce_all(send, keep, aux):
    halves = [PART >> (s + 1) for s in range(4)] + [16]
    bufs = [pltpu.VMEM((4, h, W), BF16) for h in halves]
    dma = pltpu.SemaphoreType.DMA
    return pl.pallas_call(
        reduce_kernel,
        in_specs=[pl.BlockSpec(memory_space=pltpu.VMEM)] * 3,
        out_specs=[pl.BlockSpec(memory_space=pl.ANY), pl.BlockSpec(memory_space=pltpu.VMEM)],
        out_shape=[
            jax.ShapeDtypeStruct((4, R, W), BF16),
            jax.ShapeDtypeStruct((2, 8, W), F32),
        ],
        scratch_shapes=[
            pltpu.VMEM((R, W), F32),
            pltpu.VMEM((R, W), BF16),
            *bufs,
            *bufs,
            pltpu.VMEM((4, 16, W), BF16),
            dma((5, 4)),
            dma((5, 4)),
            dma((2,)),
            dma((2,)),
            dma((5, 4)),
            dma((5, 4)),
            dma((4,)),
            dma((5,)),
            dma((5,)),
        ],
        compiler_params=pltpu.CompilerParams(
            collective_id=0, has_side_effects=True, vmem_limit_bytes=VMEM_LIMIT
        ),
        name="reduce_all",
    )(send, keep, aux)


def query_kernel(
    meta, q_ref, x_ref, ui_ref, ug_ref, uo_ref, aux_ref, auxo_ref, proj_ref,
    out_ref, ni_ref, ng_ref, no_ref, wcat, wout, total,
):
    j, t = pl.program_id(0), pl.program_id(1)
    mine = j < 2
    aux = jnp.where(mine, aux_ref[...], auxo_ref[...])

    @pl.when(t == 0)
    def _():
        for n, ref in enumerate((ui_ref, ug_ref, uo_ref)):
            moved = ref[...].astype(F32)
            scale = jnp.sqrt(aux[n : n + 1, :] + 1e-06) / jnp.sqrt(
                jnp.sum(moved * moved, axis=0, keepdims=True) + 1e-06
            )
            fresh = (moved * scale).astype(BF16)
            if n < 2:
                wcat[:, n * W : (n + 1) * W] = fresh
            else:
                wout[...] = fresh

        @pl.when(mine)
        def _():
            ni_ref[...] = wcat[:, :W]
            ng_ref[...] = wcat[:, W:]
            no_ref[...] = wout[...]

    q = jnp.where(mine, q_ref[...], x_ref[...])
    pre = dot(q, wcat[...], ((1,), (0,)))
    pre_in = pre[:, :W]
    hidden = (pre_in * jax.nn.sigmoid(pre_in) * pre[:, W:]).astype(BF16)
    head_out = dot(hidden, wout[...], ((1,), (0,)))
    inverse = lax.rsqrt(jnp.mean(head_out * head_out, axis=-1, keepdims=True) + 1e-06)
    normed = (head_out * inverse * aux[3:4, :]).astype(BF16)
    part = dot(normed, proj_ref[...], ((1,), (1,)))
    tm = part.shape[0]
    at = pl.ds(pl.multiple_of(t * tm, tm), tm)

    @pl.when(j == 0)
    def _():
        total[at, :] = part

    @pl.when((j > 0) & (j < 3))
    def _():
        total[at, :] += part

    @pl.when(j == 3)
    def _():
        out_ref[...] = (total[at, :] + part).astype(BF16)


def queries(meta, q, x, u, aux, auxo, proj, tm=256):
    tok = q.shape[0]
    steps = tok // tm
    feat = proj.shape[1]

    def head(j, m):
        own = j < 2
        return jnp.where(own, 2 * m[0] + j, 2 * (1 - m[0]) + j - 2)

    def q_map(j, t, m):
        return jnp.where(j < 2, t, steps - 1), jnp.minimum(j, 1)

    def x_map(j, t, m):
        return jnp.where(j < 2, 0, t), jnp.maximum(j - 2, 0)

    def weight(n):
        return pl.BlockSpec((None, W, W), lambda j, t, m: (head(j, m), n, 0))

    new = pl.BlockSpec((None, W, W), lambda j, t, m: (jnp.minimum(j, 1), 0, 0))
    return pl.pallas_call(
        query_kernel,
        grid_spec=pltpu.PrefetchScalarGridSpec(
            num_scalar_prefetch=1,
            grid=(4, steps),
            in_specs=[
                pl.BlockSpec((tm, W), q_map),
                pl.BlockSpec((tm, W), x_map),
                weight(0),
                weight(1),
                weight(2),
                pl.BlockSpec((None, 8, W), lambda j, t, m: (jnp.minimum(j, 1), 0, 0)),
                pl.BlockSpec((None, 8, W), lambda j, t, m: (jnp.maximum(j - 2, 0), 0, 0)),
                pl.BlockSpec(
                    (None, feat, W), lambda j, t, m: (head(j, m) // 2, 0, head(j, m) % 2)
                ),
            ],
            out_specs=[
                pl.BlockSpec((tm, feat), lambda j, t, m: (jnp.where(j == 3, t, 0), 0)),
                new,
                new,
                new,
            ],
            scratch_shapes=[
                pltpu.VMEM((W, 2 * W), BF16),
                pltpu.VMEM((W, W), BF16),
                pltpu.VMEM((tok, feat), F32),
            ],
        ),
        out_shape=[
            jax.ShapeDtypeStruct((tok, feat), BF16),
            jax.ShapeDtypeStruct((2, W, W), BF16),
            jax.ShapeDtypeStruct((2, W, W), BF16),
            jax.ShapeDtypeStruct((2, W, W), BF16),
        ],
        compiler_params=pltpu.CompilerParams(vmem_limit_bytes=VMEM_LIMIT),
        name="queries",
    )(meta, q, x, u, u, u, aux, auxo, proj)


def on_device(
    key_rows, value_rows, query_rows, learn_rates, fast_in, fast_gate, fast_out, head_gain, out_proj
):
    swapped = lax.ppermute(query_rows, "head", [(0, 1), (1, 0)])
    block = out_proj.T
    n_ctx = 2 * 4 * 4 * 2
    half = n_ctx // 2
    perm = [(2 * c + h, 2 * (h * half + c % half) + c // half) for c in range(n_ctx) for h in range(2)]
    block = lax.ppermute(block, ("ctx", "head"), perm)
    proj = lax.all_gather(block, "ctx", axis=0, tiled=True).reshape(2, -1, block.shape[1])

    core = lax.axis_index("ctx") % 2
    meta = jnp.stack([core, *final_rows()]).astype(jnp.int32)
    send, keep, aux = gradients(
        meta, key_rows, value_rows, learn_rates[:, :, None], fast_in, fast_gate, fast_out,
        head_gain.reshape(2, 1, W),
    )
    u, auxo = reduce_all(send, keep, aux)
    x_lo = lax.axis_index("head").reshape(1).astype(jnp.int32)
    return tuple(queries(x_lo, query_rows, swapped, u, aux, auxo, proj))


def solution(mesh):
    return jax.shard_map(
        on_device,
        mesh=mesh,
        in_specs=(
            P("ctx", "head"),
            P("ctx", "head"),
            P("ctx", "head"),
            P("head", "ctx"),
            P("head", None, None),
            P("head", None, None),
            P("head", None, None),
            P("head"),
            P("head", "ctx"),
        ),
        out_specs=(
            P("ctx", "head"),
            P("head", None, None),
            P("head", None, None),
            P("head", None, None),
        ),
        check_vma=False,
    )
```

time: 887 us -> 205 us (0.23)
  waiting for transfers between devices: 775 us -> 0.04 us
  Pallas kernels: 0 us -> 174 us
  matrix products: 65.3 us -> 0 us
  other arithmetic: 15 us -> 0 us
  local copies, waits for them, and re-layouts: 17 us -> 6.12 us
  starting transfers between devices: 0.12 us -> 10.2 us
    psum x1 -> x0, waiting for transfers between devices: 663 us -> none  [on_device(): sum_in, sum_gate, sum_out = lax.psum((grad_in, grad_gate, grad_out), 'ctx')]
    pallas_call x0 -> x3, Pallas kernels: none -> 174 us  [the longest x1 104 us: reduce_all(): pl.pallas_call(reduce_kernel, in_specs=[pl.BlockSpec(memory_space=pltpu.V...]
    dot_general x9 -> x0, matrix products: 65.3 us -> none  [the longest x1 12 us: on_device(): jnp.dot(normed, lax.all_gather(out_proj, 'ctx', axis=1, tiled=True), pref...]
    reduce_scatter x1 -> x0, waiting for transfers between devices: 62.3 us -> none  [on_device(): lax.psum_scatter(partial_out.astype(jnp.bfloat16), 'head', scatter_dimens...]
    all_gather x1, waiting for transfers between devices: 49.1 us -> 0.02 us  [on_device(): lax.all_gather(block, 'ctx', axis=0, tiled=True)]
    unnamed x28 -> x4, local copies, waits for them, and re-layouts: 12.6 us -> 2.12 us
    ppermute x0 -> x2, starting transfers between devices: none -> 10.1 us  [the longest x1 8.57 us: on_device(): swapped = lax.ppermute(query_rows, 'head', [(0, 1), (1, 0)])]
  transfers between devices with their start and end apart: 3 -> 3, of which waited for: 3 -> 0; matrix products, arithmetic and copies ran while one was open for 5% -> 2% of each run, Pallas kernels for 0% -> 63%
where the time goes in v1:
time: 205 us; the launch traced here: 204 us
  Pallas kernels  174 us (85%)
  between operations  14.1 us (7%)
  starting transfers between devices  10.2 us (5%)
  local copies, waits for them, and re-layouts  6.12 us (3%)
    pallas_call x1, Pallas kernels, reduce_all(): pl.pallas_call(reduce_kernel, in_specs=[pl.BlockSpec(memory_space=pltpu.V...  104 us
    pallas_call x1, Pallas kernels, queries(): pl.pallas_call(query_kernel, grid_spec=pltpu.PrefetchScalarGridSpec(num_s...  44.6 us
    pallas_call x1, Pallas kernels, gradients(): pl.pallas_call(grad_kernel, grid_spec=pltpu.PrefetchScalarGridSpec(num_sc...  25.3 us
    ppermute x1, starting transfers between devices, on_device(): swapped = lax.ppermute(query_rows, 'head', [(0, 1), (1, 0)])  8.57 us
  transfers between devices with their start and end apart: 3, of which 0 were waited for; matrix products, arithmetic and copies ran while one was open for 2% of the time, Pallas kernels for 63%

profile of v1, /device:TPU:1, one launch (start us, length us, event | category | flops | bytes accessed | tf_op | source)
XLA Modules:
  0.0 204.5 jit_solution(2991316018766059713)
XLA Ops:
  7.2 0.0 all-gather.2.cloned.1.call-start
  7.2 1.6 collective-permute-start.1
  8.8 0.0 collective-permute-done.1
  8.8 0.0 copy-start.1
  8.8 0.6 copy-done.1
  9.4 0.0 all-gather.2.cloned.1.call-update
  9.4 8.6 %collective-permute-start = (bf16[1024,1280]{1,0:T(8,128)(2,1)}, bf16[1024,1280]{1,0:T(8,128)(2,1)S(1)}, u32[]{:S(2)}, u32[]{:S(2)}) collective-permute-start(bf16[1024,1280]{1,0:T(8,128)(2,1)} %q_ref.1), channel_id=1, source_target_pairs={{0,1},{1,0},{2,3},{3,2},{4,5},{5,4},{6,7},{7,6},{8,9},{9,8},{10,11... | collective-permute-start | bytes 7864328 | tf_op jit(solution)/shard_map/ppermute | solution.py:461
  18.0 2.0 copy.13.lr_ref
  20.0 1.3 reshape.18.gain_ref
  21.3 0.7 stack.23.meta
  22.0 25.3 %gradients.1 = (bf16[2048,640]{1,0:T(8,128)(2,1)}, f32[2048,640]{1,0:T(8,128)}, f32[2,8,640]{2,1,0:T(8,128)}) custom-call(s32[5]{0:T(128)} %stack.23.meta, bf16[1024,1280]{1,0:T(8,128)(2,1)} %k_ref.1, bf16[1024,1280]{1,0:T(8,128)(2,1)} %v_ref.1, f32[2,1024,1]{2,1,0:T(8,128)} %copy.13.lr_ref, bf16[2,640,640]{2,1,0:T(8,128)(2,1)} %wi_ref.1, ...), custom_call_target="tpu_custom_call" | custom-call | flops 10066329600 | bytes 20000000 | tf_op jit(solution)/shard_map/gradients/pallas_call | solution.py:88
  47.3 104.1 %reduce_all.1 = (bf16[4,2048,640]{2,1,0:T(8,128)(2,1)}, f32[2,8,640]{2,1,0:T(8,128)}) custom-call(bf16[2048,640]{1,0:T(8,128)(2,1)} %get-tuple-element.9.send_ref, f32[2048,640]{1,0:T(8,128)} %get-tuple-element.10.keep_ref, f32[2,8,640]{2,1,0:T(8,128)} %get-tuple-element.11.aux_ref), custom_call_target="tpu_custom_call" | custom-call | tf_op jit(solution)/shard_map/reduce_all/pallas_call | solution.py:317
  151.5 0.0 collective-permute-done.x_ref
  151.5 0.0 copy-start
  151.5 0.0 all-gather.2.cloned.1.call-done
  151.5 1.5 copy-done
  153.0 44.6 %queries.1 = (bf16[1024,1280]{1,0:T(8,128)(2,1)}, bf16[2,640,640]{2,1,0:T(8,128)(2,1)}, bf16[2,640,640]{2,1,0:T(8,128)(2,1)}, bf16[2,640,640]{2,1,0:T(8,128)(2,1)}) custom-call(s32[1]{0:T(128)} %bitcast.meta, bf16[1024,1280]{1,0:T(8,128)(2,1)} %q_ref.1, bf16[1024,1280]{1,0:T(8,128)(2,1)} %copy-done, ...), custom_call_target="tpu_custom_call" | custom-call | tf_op jit(solution)/shard_map/queries/pallas_call | solution.py:418
Async XLA Ops:
  7.2 144.4 %all-gather.2.cloned.1.call-start = ((), (), s32[]{:S(2)}) async-start(), calls=%async_computation | async-start | bytes 6656000 | tf_op jit(solution)/shard_map/all_gather | solution.py:467
  7.2 1.6 collective-permute-start.1
  8.8 0.6 copy-start.1
  9.4 142.0 %collective-permute-start = (bf16[1024,1280]{1,0:T(8,128)(2,1)}, bf16[1024,1280]{1,0:T(8,128)(2,1)S(1)}, u32[]{:S(2)}, u32[]{:S(2)}) collective-permute-start(bf16[1024,1280]{1,0:T(8,128)(2,1)} %q_ref.1), channel_id=1, source_target_pairs={{0,1},{1,0},{2,3},{3,2},{4,5},{5,4},{6,7},{7,6},{8,9},{9,8},{10,11... | collective-permute-start | bytes 7864328 | tf_op jit(solution)/shard_map/ppermute | solution.py:461
  151.5 1.5 copy-start
Sparse Core Ops, SparseCore 0:
  11.6 98.3 all-gather.1

commit v2 on v1

v2 whole, which is shorter than its diff:
```python
import functools

import jax
import jax.numpy as jnp
from jax import lax
from jax.experimental import pallas as pl
from jax.experimental.pallas import tpu as pltpu
from jax.sharding import PartitionSpec as P

MESH = pl.DeviceIdType.MESH
W = 640
R = 2048
PART = R // 4
F32 = jnp.float32
BF16 = jnp.bfloat16
VMEM_LIMIT = 60 * 1024 * 1024


def dot(a, b, dims):
    return lax.dot_general(a, b, ((dims[0], dims[1]), ((), ())), preferred_element_type=F32)


def position():
    ctx, x_lo = lax.axis_index("ctx"), lax.axis_index("head")
    core, x_hi = ctx % 2, (ctx // 2) % 2
    y, z = (ctx // 4) % 4, ctx // 16
    return z, y, x_hi, core, x_lo


def ctx_of(z, y, x_hi, core):
    return ((z * 4 + y) * 2 + x_hi) * 2 + core


def bits_of(z, y):
    return ((y + 1) // 2) % 2, ((z + 1) // 2) % 2, y // 2, z // 2


def flip(r):
    return r + 1 - 2 * (r % 2)


def final_rows():
    z, y, x_hi, _, _ = position()
    bits = bits_of(z, y)
    rows = []
    for part in range(4):
        base = part * PART
        for step in range(4):
            base = base + bits[(part + step) % 4] * (PART >> (step + 1))
        rows.append(base + x_hi * 16)
    return rows


TM = 512
CH = 64


def rows_loop(count, fn):
    step = min(count, CH)

    def body(n, carry):
        fn(pl.multiple_of(n * step, step), step)
        return carry

    if count == step:
        fn(0, step)
    else:
        lax.fori_loop(0, count // step, body, 0)


def rows(start, size, align=16):
    return pl.ds(pl.multiple_of(start, align), size)


def reduce_kernel(
    k_hbm, v_hbm, q_hbm, lr_ref, wi_hbm, wg_hbm, wo_hbm, gain_ref, proj_hbm,
    u_ref, q_out, t_ref, aux_ref, auxo_ref,
    kbuf, vbuf, wcat, wout, acc, send, core_buf, s0, s1, s2, s3, s4, r0, r1, r2, r3, r4, shard,
    ld_sem, s_sem, r_sem, m_ssem, m_rsem, t_ssem, t_rsem, f_ssem, f_rsem, g_ssem, g_rsem,
    fw_ssem, fw_rsem, l_sem,
):
    z, y, x_hi, core, x_lo = position()
    bits = bits_of(z, y)
    peers = (
        (ctx_of(z, flip(y), x_hi, core), x_lo),
        (ctx_of(flip(z), y, x_hi, core), x_lo),
        (ctx_of(z, 3 - y, x_hi, core), x_lo),
        (ctx_of(3 - z, y, x_hi, core), x_lo),
    )
    far = (ctx_of(z, y, 1 - x_hi, core), x_lo)
    mate = (ctx_of(z, y, x_hi, 1 - core), x_lo)
    side = (ctx_of(z, y, x_hi, core), 1 - x_lo)
    cross = (ctx_of(z, y, 1 - x_hi, core), 1 - x_lo)
    y_opp = (ctx_of(z, (y + 2) % 4, x_hi, core), x_lo)
    z_opp = (ctx_of((z + 2) % 4, y, x_hi, core), x_lo)
    swap = (ctx_of((z + 2) % 4, y, x_hi, core), 1 - x_lo)

    barrier = pltpu.get_barrier_semaphore()
    everyone = (*peers, far, mate, side, cross, y_opp, z_opp, swap)
    for dev in everyone:
        pl.semaphore_signal(barrier, inc=1, device_id=dev, device_id_type=MESH)

    def remote(src, dst, ssem, rsem, dev):
        return pltpu.make_async_remote_copy(
            src_ref=src, dst_ref=dst, send_sem=ssem, recv_sem=rsem,
            device_id=dev, device_id_type=MESH,
        )

    loads = []
    for i in range(2):
        h = 1 - core if i == 0 else core
        cols = pl.ds(pl.multiple_of(h * W, 128), W)
        tile = pl.ds(0, TM), pl.ds(TM, TM)
        pairs = (
            (wi_hbm.at[h], wcat.at[i, :, pl.ds(0, W)]),
            (wg_hbm.at[h], wcat.at[i, :, pl.ds(W, W)]),
            (k_hbm.at[tile[0], cols], kbuf.at[i, tile[0]]),
            (v_hbm.at[tile[0], cols], vbuf.at[i, tile[0]]),
            (wo_hbm.at[h], wout.at[i]),
            (k_hbm.at[tile[1], cols], kbuf.at[i, tile[1]]),
            (v_hbm.at[tile[1], cols], vbuf.at[i, tile[1]]),
        )
        loads.append([pltpu.make_async_copy(a, b, ld_sem.at[i, n]) for n, (a, b) in enumerate(pairs)])
        for copy in loads[-1]:
            copy.start()
    pl.semaphore_wait(barrier, len(everyone))

    q_copy = remote(q_hbm, q_out, m_ssem.at[0], m_rsem.at[0], side)
    q_copy.start()

    stays = x_lo == z // 2
    home = jnp.where(stays, z, (z + 2) % 4)
    t_swap = remote(proj_hbm, t_ref.at[(z + 2) % 4, y, x_hi, core], t_ssem.at[0], t_rsem.at[0], swap)
    t_keep = pltpu.make_async_copy(proj_hbm, t_ref.at[z, y, x_hi, core], l_sem.at[0])

    @pl.when(jnp.logical_not(stays))
    def _():
        t_swap.start()

    @pl.when(stays)
    def _():
        t_keep.start()

    t_far = remote(
        t_ref.at[z, y, x_hi, core], t_ref.at[z, y, x_hi, core], t_ssem.at[1], t_rsem.at[1], far
    )

    def line(d, first):
        along_y = core == 0 if first else core == 1
        dev_y = (ctx_of(z, (y + d) % 4, x_hi, core), x_lo)
        dev_z = (ctx_of((z + d) % 4, y, x_hi, core), x_lo)
        dev = jnp.where(along_y, dev_y[0], dev_z[0]), x_lo
        n = 1 + d if first else 4 + d
        return dev, t_ssem.at[n], t_rsem.at[n]

    t_one = []
    for d in (1, 3, 2):
        dev, ssem, rsem = line(d, True)
        block = t_ref.at[z, y, :, core]
        t_one.append(remote(block, block, ssem, rsem, dev))
    t_two_y, t_two_z = [], []
    for d in (1, 3, 2):
        dev, ssem, rsem = line(d, False)
        row = t_ref.at[z, :, :, core]
        col = t_ref.at[:, y, :, core]
        t_two_z.append(remote(row, row, ssem, rsem, dev))
        t_two_y.append(remote(col, col, ssem, rsem, dev))
    t_all = t_ref.at[:, :, :, core]
    t_mate = remote(t_all, t_all, t_ssem.at[8], t_rsem.at[8], mate)

    head_swap = remote(send, core_buf, m_ssem.at[1], m_rsem.at[1], mate)

    def tile_step(n, carry):
        i, t = n // 2, n % 2
        for m in range(4):

            @pl.when(n == m)
            def _():
                for copy in loads[m // 2][0:5] if m % 2 == 0 else loads[m // 2][5:7]:
                    copy.wait()

        at = rows(t * TM, TM, TM)
        k = kbuf[i, at, :]
        pre = dot(k, wcat[i], ((1,), (0,)))
        pre_in, pre_gate = pre[:, :W], pre[:, W:]
        sig = jax.nn.sigmoid(pre_in)
        act = pre_in * sig
        hidden = (act * pre_gate).astype(BF16)
        h = jnp.where(i == 0, 1 - core, core)
        lr = lr_ref[pl.ds(h, 1), at]
        lr = jnp.transpose(jnp.broadcast_to(lr, (128, TM)))
        err = (jnp.concatenate([lr] * 5, axis=1) * vbuf[i, at, :].astype(F32)).astype(BF16)
        back = dot(err, wout[i], ((1,), (1,)))
        back_in = (back * pre_gate * sig * (1.0 + pre_in * (1.0 - sig))).astype(BF16)
        back_gate = (back * act).astype(BF16)
        gcat = dot(k, jnp.concatenate([back_in, back_gate], axis=1), ((0,), (0,)))
        grads = gcat[:, :W], gcat[:, W:], dot(hidden, err, ((0,), (0,)))
        for m, grad in enumerate(grads):
            to = pl.ds(m * W, W)

            @pl.when(t == 0)
            def _():
                acc[to, :] = grad

            @pl.when(n == 1)
            def _():
                send[to, :] = (acc[to, :] + grad).astype(BF16)

            @pl.when(n == 3)
            def _():
                acc[to, :] += grad

        @pl.when(n == 0)
        def _():
            @pl.when(stays)
            def _():
                t_keep.wait()

            @pl.when(jnp.logical_not(stays))
            def _():
                t_swap.wait()

            t_far.start()

        @pl.when(n == 1)
        def _():
            send[3 * W :, :] = jnp.zeros((R - 3 * W, W), BF16)
            acc[3 * W :, :] = jnp.zeros((R - 3 * W, W), F32)
            head_swap.start()
            t_far.wait()
            for copy in t_one:
                copy.start()

        @pl.when(n == 2)
        def _():
            for copy in t_one:
                copy.wait()

            @pl.when(core == 0)
            def _():
                for copy in t_two_z:
                    copy.start()

            @pl.when(core == 1)
            def _():
                for copy in t_two_y:
                    copy.start()

        return carry

    lax.fori_loop(0, 4, tile_step, 0)

    finals = final_rows()
    for p in range(4):
        for n in range(3):

            @pl.when((finals[p] >= n * W) & (finals[p] < (n + 1) * W))
            def _():
                at = rows(finals[p] - n * W, 16)
                weight = wcat[1, at, n * W : (n + 1) * W] if n < 2 else wout[1, at, :]
                acc[rows(finals[p], 16), :] += weight.astype(F32)

    head_swap.wait_recv()
    sbuf, rbuf = (s0, s1, s2, s3, s4), (r0, r1, r2, r3, r4)
    base = [p * PART for p in range(4)]
    copies = [[None] * 4 for _ in range(5)]
    for step in range(5):
        half = (PART >> (step + 1)) if step < 4 else 16
        kept_at = [None] * 4
        for p in range(4):
            d = (p + step) % 4
            bit = bits[d] if step < 4 else x_hi
            out_at = base[p] + (1 - bit) * half
            kept_at[p] = base[p] + bit * half
            if step > 0:
                copies[step - 1][p].wait_recv()
            got_ref = core_buf if step == 0 else rbuf[step - 1].at[p]
            got_at = out_at if step == 0 else (1 - bit) * half
            into = sbuf[step].at[p]

            def emit(o, size, out_at=out_at, got_at=got_at, into=into, got_ref=got_ref):
                into[rows(o, size), :] = (
                    acc[rows(out_at + o, size), :] + got_ref[rows(got_at + o, size), :].astype(F32)
                ).astype(BF16)

            rows_loop(half, emit)
            copies[step][p] = remote(
                sbuf[step].at[p], rbuf[step].at[p], s_sem.at[step, p], r_sem.at[step, p],
                peers[d] if step < 4 else far,
            )
            copies[step][p].start()
        for p in range(4):
            bit = bits[(p + step) % 4] if step < 4 else x_hi
            got_ref = core_buf if step == 0 else rbuf[step - 1].at[p]
            got_at = kept_at[p] if step == 0 else bit * half

            def hold(o, size, at0=kept_at[p], got_at=got_at, got_ref=got_ref):
                at = rows(at0 + o, size)
                acc[at, :] = acc[at, :] + got_ref[rows(got_at + o, size), :].astype(F32)

            rows_loop(half, hold)
            base[p] = kept_at[p]
        if step == 0:
            for d in range(3):

                @pl.when(core == 0)
                def _():
                    t_two_z[d].wait()

                @pl.when(core == 1)
                def _():
                    t_two_y[d].wait()

            t_mate.start()
            for i in range(2):
                h = 1 - core if i == 0 else core
                aux_ref[h] = jnp.zeros((8, W), F32)
                for n in range(3):
                    wide = (wcat[i, :, n * W : (n + 1) * W] if n < 2 else wout[i]).astype(F32)
                    aux_ref[h, n : n + 1, :] = jnp.sum(wide * wide, axis=0, keepdims=True)
            for h in range(2):
                aux_ref[h, 3:4, :] = gain_ref[h * W : (h + 1) * W].reshape(1, W)
            aux_copy = remote(aux_ref, auxo_ref, m_ssem.at[2], m_rsem.at[2], side)
            aux_copy.start()

    own, other = 2 * x_lo + core, 2 * (1 - x_lo) + core
    locals_, firsts = [], []
    for p in range(4):
        copies[4][p].wait_recv()
        shard[p, :, :] = (acc[rows(base[p], 16), :] + r4[p, :, :].astype(F32)).astype(BF16)
        dst = u_ref.at[own, rows(base[p], 16)]
        for n, dev in enumerate((far, side, cross)):
            copy = remote(shard.at[p], dst, f_ssem.at[n, p], f_rsem.at[n, p], dev)
            copy.start()
            firsts.append(copy)
        local = pltpu.make_async_copy(shard.at[p], dst, l_sem.at[1 + p])
        local.start()
        locals_.append(local)
        base[p] = base[p] - x_hi * 16
    for copy in locals_:
        copy.wait()
    for copy in firsts:
        copy.wait_recv()
    gathers, forwards = [], []
    waiting = [[] for _ in range(4)]
    size = 32
    for step in range(3, -1, -1):
        parts = 2 if step == 0 else 1
        piece = size // parts
        arrived = [list(w) for w in waiting]
        waiting = [[] for _ in range(4)]
        for p in range(4):
            for copy in arrived[p]:
                copy.wait_recv()
        for g, head in enumerate((own, other)):
            for c in range(parts):
                for p in range(4):
                    d = (p + step) % 4
                    block = u_ref.at[head, rows(base[p] + c * piece, piece, 32)]
                    sem = (g, 4 * (step + c) + p) if step == 0 else (g, 4 * (step + 1) + p)
                    copy = remote(block, block, g_ssem.at[sem], g_rsem.at[sem], peers[d])
                    copy.start()
                    gathers.append(copy)
                    waiting[p].append(copy)
        if step == 0:
            n = 0
            for head in (own, other):
                for p in range(4):
                    block = u_ref.at[head, rows(base[p], size, 32)]
                    copy = remote(block, block, fw_ssem.at[n], fw_rsem.at[n], mate)
                    copy.start()
                    forwards.append(copy)
                    n += 1
            for g, head in enumerate((own, other)):
                for c in range(2):
                    for p in range(4):
                        waiting[p][2 * g + c].wait_recv()
                        theirs = base[p] + (1 - 2 * bits[p]) * size
                        block = u_ref.at[head, rows(theirs + c * piece, piece, 32)]
                        copy = remote(block, block, fw_ssem.at[n], fw_rsem.at[n], mate)
                        copy.start()
                        forwards.append(copy)
                        n += 1
        for p in range(4):
            base[p] = base[p] - bits[(p + step) % 4] * size
        size *= 2
    for copy in forwards:
        copy.wait_recv()
    q_copy.wait()
    aux_copy.wait()
    t_mate.wait()
    head_swap.wait_send()
    for copy in (*forwards, *gathers, *firsts):
        copy.wait_send()
    for step in range(5):
        for p in range(4):
            copies[step][p].wait_send()


def reduce_all(k, v, q, lr, wi, wg, wo, gain, proj):
    tok = k.shape[0]
    halves = [PART >> (s + 1) for s in range(4)] + [16]
    bufs = [pltpu.VMEM((4, h, W), BF16) for h in halves]
    dma = pltpu.SemaphoreType.DMA
    hbm = pl.BlockSpec(memory_space=pl.ANY)
    vmem = pl.BlockSpec(memory_space=pltpu.VMEM)
    return pl.pallas_call(
        reduce_kernel,
        in_specs=[hbm, hbm, hbm, vmem, hbm, hbm, hbm, vmem, hbm],
        out_specs=[hbm, hbm, hbm, vmem, vmem],
        out_shape=[
            jax.ShapeDtypeStruct((4, R, W), BF16),
            jax.ShapeDtypeStruct(q.shape, BF16),
            jax.ShapeDtypeStruct((4, 4, 2, 2, *proj.shape), BF16),
            jax.ShapeDtypeStruct((2, 8, W), F32),
            jax.ShapeDtypeStruct((2, 8, W), F32),
        ],
        scratch_shapes=[
            pltpu.VMEM((2, tok, W), BF16),
            pltpu.VMEM((2, tok, W), BF16),
            pltpu.VMEM((2, W, 2 * W), BF16),
            pltpu.VMEM((2, W, W), BF16),
            pltpu.VMEM((R, W), F32),
            pltpu.VMEM((R, W), BF16),
            pltpu.VMEM((R, W), BF16),
            *bufs,
            *bufs,
            pltpu.VMEM((4, 16, W), BF16),
            dma((2, 7)),
            dma((5, 4)),
            dma((5, 4)),
            dma((3,)),
            dma((3,)),
            dma((9,)),
            dma((9,)),
            dma((3, 4)),
            dma((3, 4)),
            dma((2, 20)),
            dma((2, 20)),
            dma((24,)),
            dma((24,)),
            dma((5,)),
        ],
        compiler_params=pltpu.CompilerParams(
            collective_id=0, has_side_effects=True, vmem_limit_bytes=VMEM_LIMIT
        ),
        name="reduce_all",
    )(k, v, q, lr, wi, wg, wo, gain, proj)


def query_kernel(
    meta, q_ref, x_ref, ui_ref, ug_ref, uo_ref, aux_ref, auxo_ref, proj_ref,
    out_ref, ni_ref, ng_ref, no_ref, wcat, wout, total,
):
    j, t = pl.program_id(0), pl.program_id(1)
    mine = j < 2
    aux = jnp.where(mine, aux_ref[...], auxo_ref[...])

    @pl.when(t == 0)
    def _():
        for n, ref in enumerate((ui_ref, ug_ref, uo_ref)):
            moved = ref[...].astype(F32)
            scale = jnp.sqrt(aux[n : n + 1, :] + 1e-06) / jnp.sqrt(
                jnp.sum(moved * moved, axis=0, keepdims=True) + 1e-06
            )
            fresh = (moved * scale).astype(BF16)
            if n < 2:
                wcat[:, n * W : (n + 1) * W] = fresh
            else:
                wout[...] = fresh

        @pl.when(mine)
        def _():
            ni_ref[...] = wcat[:, :W]
            ng_ref[...] = wcat[:, W:]
            no_ref[...] = wout[...]

    q = jnp.where(mine, q_ref[...], x_ref[...])
    pre = dot(q, wcat[...], ((1,), (0,)))
    pre_in = pre[:, :W]
    hidden = (pre_in * jax.nn.sigmoid(pre_in) * pre[:, W:]).astype(BF16)
    head_out = dot(hidden, wout[...], ((1,), (0,)))
    inverse = lax.rsqrt(jnp.mean(head_out * head_out, axis=-1, keepdims=True) + 1e-06)
    normed = (head_out * inverse * aux[3:4, :]).astype(BF16)
    part = dot(normed, proj_ref[...], ((1,), (1,)))
    tm = part.shape[0]
    at = pl.ds(pl.multiple_of(t * tm, tm), tm)

    @pl.when(j == 0)
    def _():
        total[at, :] = part

    @pl.when((j > 0) & (j < 3))
    def _():
        total[at, :] += part

    @pl.when(j == 3)
    def _():
        out_ref[...] = (total[at, :] + part).astype(BF16)


def queries(meta, q, x, u, aux, auxo, proj, tm=1024):
    tok = q.shape[0]
    steps = tok // tm
    feat = proj.shape[1]

    def head(j, m):
        own = j < 2
        return jnp.where(own, 2 * m[0] + j, 2 * (1 - m[0]) + j - 2)

    def q_map(j, t, m):
        return jnp.where(j < 2, t, steps - 1), jnp.minimum(j, 1)

    def x_map(j, t, m):
        return jnp.where(j < 2, 0, t), jnp.maximum(j - 2, 0)

    def weight(n):
        return pl.BlockSpec((None, W, W), lambda j, t, m: (head(j, m), n, 0))

    new = pl.BlockSpec((None, W, W), lambda j, t, m: (jnp.minimum(j, 1), 0, 0))
    return pl.pallas_call(
        query_kernel,
        grid_spec=pltpu.PrefetchScalarGridSpec(
            num_scalar_prefetch=1,
            grid=(4, steps),
            in_specs=[
                pl.BlockSpec((tm, W), q_map),
                pl.BlockSpec((tm, W), x_map),
                weight(0),
                weight(1),
                weight(2),
                pl.BlockSpec((None, 8, W), lambda j, t, m: (jnp.minimum(j, 1), 0, 0)),
                pl.BlockSpec((None, 8, W), lambda j, t, m: (jnp.maximum(j - 2, 0), 0, 0)),
                pl.BlockSpec(
                    (None, feat, W), lambda j, t, m: (head(j, m) // 2, 0, head(j, m) % 2)
                ),
            ],
            out_specs=[
                pl.BlockSpec((tm, feat), lambda j, t, m: (jnp.where(j == 3, t, 0), 0)),
                new,
                new,
                new,
            ],
            scratch_shapes=[
                pltpu.VMEM((W, 2 * W), BF16),
                pltpu.VMEM((W, W), BF16),
                pltpu.VMEM((tok, feat), F32),
            ],
        ),
        out_shape=[
            jax.ShapeDtypeStruct((tok, feat), BF16),
            jax.ShapeDtypeStruct((2, W, W), BF16),
            jax.ShapeDtypeStruct((2, W, W), BF16),
            jax.ShapeDtypeStruct((2, W, W), BF16),
        ],
        compiler_params=pltpu.CompilerParams(vmem_limit_bytes=VMEM_LIMIT),
        name="queries",
    )(meta, q, x, u, u, u, aux, auxo, proj)


def on_device(
    key_rows, value_rows, query_rows, learn_rates, fast_in, fast_gate, fast_out, head_gain, out_proj
):
    u, swapped, proj, aux, auxo = reduce_all(
        key_rows, value_rows, query_rows, learn_rates, fast_in, fast_gate, fast_out, head_gain,
        out_proj.T,
    )
    proj = proj.reshape(2, -1, proj.shape[-1])
    x_lo = lax.axis_index("head").reshape(1).astype(jnp.int32)
    return tuple(queries(x_lo, query_rows, swapped, u, aux, auxo, proj))


def solution(mesh):
    return jax.shard_map(
        on_device,
        mesh=mesh,
        in_specs=(
            P("ctx", "head"),
            P("ctx", "head"),
            P("ctx", "head"),
            P("head", "ctx"),
            P("head", None, None),
            P("head", None, None),
            P("head", None, None),
            P("head"),
            P("head", "ctx"),
        ),
        out_specs=(
            P("ctx", "head"),
            P("head", None, None),
            P("head", None, None),
            P("head", None, None),
        ),
        check_vma=False,
    )
```

time: 205 us -> 207 us (level)
  Pallas kernels: 174 us -> 206 us
  between operations: 14.1 us -> 0.72 us
  starting transfers between devices: 10.2 us -> 0 us
  local copies, waits for them, and re-layouts: 6.12 us -> 0 us
    pallas_call x2 -> x1, Pallas kernels: 129 us -> 168 us  [reduce_all(): pl.pallas_call(reduce_kernel, in_specs=[hbm, hbm, hbm, vmem, hbm, hbm, hb...]
    ppermute x2 -> x0, starting transfers between devices: 10.1 us -> none  [the longest x1 8.57 us: on_device(): swapped = lax.ppermute(query_rows, 'head', [(0, 1), (1, 0)])]
    pallas_call x1, Pallas kernels: 44.6 us -> 38 us  [queries(): pl.pallas_call(query_kernel, grid_spec=pltpu.PrefetchScalarGridSpec(num_s...]
    unnamed x4 -> x0, local copies, waits for them, and re-layouts: 2.12 us -> none
  transfers between devices with their start and end apart: 3 -> 0, of which waited for: 0 -> 0; matrix products, arithmetic and copies ran while one was open for 2% -> 0% of each run, Pallas kernels for 63% -> 0%
where the time goes in v2:
time: 207 us; the launch traced here: 206 us
  Pallas kernels  206 us (100%)
    pallas_call x1, Pallas kernels, reduce_all(): pl.pallas_call(reduce_kernel, in_specs=[hbm, hbm, hbm, vmem, hbm, hbm, hb...  168 us
    pallas_call x1, Pallas kernels, queries(): pl.pallas_call(query_kernel, grid_spec=pltpu.PrefetchScalarGridSpec(num_s...  38 us

profile of v2, /device:TPU:1, one launch (start us, length us, event | category | flops | bytes accessed | tf_op | source)
XLA Modules:
  0.0 206.4 jit_solution(1465751702990201267)
XLA Ops:
  0.6 167.7 %reduce_all.1 = (bf16[4,2048,640]{2,1,0:T(8,128)(2,1)}, bf16[1024,1280]{1,0:T(8,128)(2,1)}, bf16[4,4,2,2,40,1280]{5,4,3,2,1,0:T(8,128)(2,1)}, f32[2,8,640]{2,1,0:T(8,128)}, f32[2,8,640]{2,1,0:T(8,128)}) custom-call(bf16[1024,1280]{1,0:T(8,128)(2,1)} %k_hbm.1, bf16[1024,1280]{1,0:T(8,128)(2,1)} %v_hbm.1, bf16[1024,1280]{1,0:T(8,128)(2,1)} %q_ref.1, ...), custom_call_target="tpu_custom_call" | custom-call | tf_op jit(solution)/shard_map/reduce_all/pallas_call | solution.py:407
  168.3 38.0 %queries.1 = (bf16[1024,1280]{1,0:T(8,128)(2,1)}, bf16[2,640,640]{2,1,0:T(8,128)(2,1)}, bf16[2,640,640]{2,1,0:T(8,128)(2,1)}, bf16[2,640,640]{2,1,0:T(8,128)(2,1)}) custom-call(s32[1]{0:T(128)} %bitcast.meta, bf16[1024,1280]{1,0:T(8,128)(2,1)} %q_ref.1, bf16[1024,1280]{1,0:T(8,128)(2,1)} %get-tuple-element.9.x_ref, ...), custom_call_target="tpu_custom_call" | custom-call | tf_op jit(solution)/shard_map/queries/pallas_call | solution.py:521

commit v3 on v2

--- a/solution.py
+++ b/solution.py
@@ -76,7 +76,7 @@
     k_hbm, v_hbm, q_hbm, lr_ref, wi_hbm, wg_hbm, wo_hbm, gain_ref, proj_hbm,
     u_ref, q_out, t_ref, aux_ref, auxo_ref,
     kbuf, vbuf, wcat, wout, acc, send, core_buf, s0, s1, s2, s3, s4, r0, r1, r2, r3, r4, shard,
-    ld_sem, s_sem, r_sem, m_ssem, m_rsem, t_ssem, t_rsem, f_ssem, f_rsem, g_ssem, g_rsem,
+    ld_sem, s_sem, r_sem, m_ssem, m_rsem, q_ssem, q_rsem, t_ssem, t_rsem, f_ssem, f_rsem, g_ssem, g_rsem,
     fw_ssem, fw_rsem, l_sem,
 ):
     z, y, x_hi, core, x_lo = position()
@@ -94,9 +94,10 @@
     y_opp = (ctx_of(z, (y + 2) % 4, x_hi, core), x_lo)
     z_opp = (ctx_of((z + 2) % 4, y, x_hi, core), x_lo)
     swap = (ctx_of((z + 2) % 4, y, x_hi, core), 1 - x_lo)
+    swap_far = (ctx_of((z + 2) % 4, y, 1 - x_hi, core), 1 - x_lo)
 
     barrier = pltpu.get_barrier_semaphore()
-    everyone = (*peers, far, mate, side, cross, y_opp, z_opp, swap)
+    everyone = (*peers, far, mate, side, cross, y_opp, z_opp, swap, swap_far)
     for dev in everyone:
         pl.semaphore_signal(barrier, inc=1, device_id=dev, device_id_type=MESH)
 
@@ -125,48 +126,65 @@
             copy.start()
     pl.semaphore_wait(barrier, len(everyone))
 
-    q_copy = remote(q_hbm, q_out, m_ssem.at[0], m_rsem.at[0], side)
-    q_copy.start()
-
     stays = x_lo == z // 2
-    home = jnp.where(stays, z, (z + 2) % 4)
-    t_swap = remote(proj_hbm, t_ref.at[(z + 2) % 4, y, x_hi, core], t_ssem.at[0], t_rsem.at[0], swap)
-    t_keep = pltpu.make_async_copy(proj_hbm, t_ref.at[z, y, x_hi, core], l_sem.at[0])
+    t_own = t_ref.at[z, y, x_hi, core]
+    t_far_slot = t_ref.at[(z + 2) % 4, y, x_hi, core]
+    t_keep = pltpu.make_async_copy(proj_hbm, t_own, l_sem.at[0])
+    t_first = remote(proj_hbm, t_own, t_ssem.at[1], t_rsem.at[1], far)
+    t_swap = remote(proj_hbm, t_far_slot, t_ssem.at[0], t_rsem.at[0], swap)
+    t_swap_far = remote(proj_hbm, t_far_slot, t_ssem.at[1], t_rsem.at[1], swap_far)
+
+    @pl.when(stays)
+    def _():
+        t_first.start()
+        t_keep.start()
 
     @pl.when(jnp.logical_not(stays))
     def _():
         t_swap.start()
-
-    @pl.when(stays)
-    def _():
-        t_keep.start()
-
-    t_far = remote(
-        t_ref.at[z, y, x_hi, core], t_ref.at[z, y, x_hi, core], t_ssem.at[1], t_rsem.at[1], far
-    )
-
-    def line(d, first):
-        along_y = core == 0 if first else core == 1
-        dev_y = (ctx_of(z, (y + d) % 4, x_hi, core), x_lo)
-        dev_z = (ctx_of((z + d) % 4, y, x_hi, core), x_lo)
-        dev = jnp.where(along_y, dev_y[0], dev_z[0]), x_lo
-        n = 1 + d if first else 4 + d
-        return dev, t_ssem.at[n], t_rsem.at[n]
+        t_swap_far.start()
+
+    def ring(d, first):
+        y_turn = core == 0 if first else core == 1
+        dev_y, dev_z = ctx_of(z, (y + d) % 4, x_hi, core), ctx_of((z + d) % 4, y, x_hi, core)
+        return jnp.where(y_turn, dev_y, dev_z), x_lo
 
     t_one = []
     for d in (1, 3, 2):
-        dev, ssem, rsem = line(d, True)
         block = t_ref.at[z, y, :, core]
-        t_one.append(remote(block, block, ssem, rsem, dev))
-    t_two_y, t_two_z = [], []
-    for d in (1, 3, 2):
-        dev, ssem, rsem = line(d, False)
-        row = t_ref.at[z, :, :, core]
-        col = t_ref.at[:, y, :, core]
-        t_two_z.append(remote(row, row, ssem, rsem, dev))
-        t_two_y.append(remote(col, col, ssem, rsem, dev))
+        t_one.append(remote(block, block, t_ssem.at[1 + d], t_rsem.at[1 + d], ring(d, True)))
+    t_two = [[], []]
+    for v in range(2):
+        for n, d in enumerate((1, 3)):
+            line = t_ref.at[z, :, :, core] if v == 0 else t_ref.at[:, y, :, core]
+            t_two[v].append(remote(line, line, t_ssem.at[5 + n], t_rsem.at[5 + n], ring(d, False)))
+    t_three = [[], []]
+    for v in range(2):
+        for n, d in enumerate((1, 3)):
+            part = pl.ds(2 * n, 2)
+            came = (4 - d) % 4
+            line = (
+                t_ref.at[(z + came) % 4, part, :, core]
+                if v == 0
+                else t_ref.at[part, (y + came) % 4, :, core]
+            )
+            t_three[v].append(remote(line, line, t_ssem.at[7 + n], t_rsem.at[7 + n], ring(d, False)))
     t_all = t_ref.at[:, :, :, core]
-    t_mate = remote(t_all, t_all, t_ssem.at[8], t_rsem.at[8], mate)
+    t_mate = remote(t_all, t_all, t_ssem.at[9], t_rsem.at[9], mate)
+
+    def by_core(copies, act):
+        for v in range(2):
+
+            @pl.when(core == v)
+            def _():
+                for copy in copies[v]:
+                    act(copy)
+
+    q_rows = q_hbm.shape[0] // 8
+    q_copies = []
+    for n in range(8):
+        at = pl.ds(n * q_rows, q_rows)
+        q_copies.append(remote(q_hbm.at[at], q_out.at[at], q_ssem.at[n], q_rsem.at[n], side))
 
     head_swap = remote(send, core_buf, m_ssem.at[1], m_rsem.at[1], mate)
 
@@ -215,36 +233,29 @@
             @pl.when(stays)
             def _():
                 t_keep.wait()
+                t_first.wait()
 
             @pl.when(jnp.logical_not(stays))
             def _():
                 t_swap.wait()
-
-            t_far.start()
+                t_swap_far.wait()
+
+            for copy in t_one:
+                copy.start()
+            for copy in q_copies[:3]:
+                copy.start()
 
         @pl.when(n == 1)
         def _():
             send[3 * W :, :] = jnp.zeros((R - 3 * W, W), BF16)
             acc[3 * W :, :] = jnp.zeros((R - 3 * W, W), F32)
             head_swap.start()
-            t_far.wait()
-            for copy in t_one:
-                copy.start()
 
         @pl.when(n == 2)
         def _():
             for copy in t_one:
                 copy.wait()
-
-            @pl.when(core == 0)
-            def _():
-                for copy in t_two_z:
-                    copy.start()
-
-            @pl.when(core == 1)
-            def _():
-                for copy in t_two_y:
-                    copy.start()
+            by_core(t_two, lambda copy: copy.start())
 
         return carry
 
@@ -301,17 +312,8 @@
             rows_loop(half, hold)
             base[p] = kept_at[p]
         if step == 0:
-            for d in range(3):
-
-                @pl.when(core == 0)
-                def _():
-                    t_two_z[d].wait()
-
-                @pl.when(core == 1)
-                def _():
-                    t_two_y[d].wait()
-
-            t_mate.start()
+            for copy in q_copies[3:5]:
+                copy.start()
             for i in range(2):
                 h = 1 - core if i == 0 else core
                 aux_ref[h] = jnp.zeros((8, W), F32)
@@ -320,8 +322,14 @@
                     aux_ref[h, n : n + 1, :] = jnp.sum(wide * wide, axis=0, keepdims=True)
             for h in range(2):
                 aux_ref[h, 3:4, :] = gain_ref[h * W : (h + 1) * W].reshape(1, W)
-            aux_copy = remote(aux_ref, auxo_ref, m_ssem.at[2], m_rsem.at[2], side)
+            aux_copy = remote(aux_ref, auxo_ref, m_ssem.at[0], m_rsem.at[0], side)
             aux_copy.start()
+        if step == 1:
+            by_core(t_two, lambda copy: copy.wait())
+            by_core(t_three, lambda copy: copy.start())
+        if step == 4:
+            by_core(t_three, lambda copy: copy.wait())
+            t_mate.start()
 
     own, other = 2 * x_lo + core, 2 * (1 - x_lo) + core
     locals_, firsts = [], []
@@ -341,6 +349,8 @@
         copy.wait()
     for copy in firsts:
         copy.wait_recv()
+    for copy in q_copies[5:]:
+        copy.start()
     gathers, forwards = [], []
     waiting = [[] for _ in range(4)]
     size = 32
@@ -386,7 +396,8 @@
         size *= 2
     for copy in forwards:
         copy.wait_recv()
-    q_copy.wait()
+    for copy in q_copies:
+        copy.wait()
     aux_copy.wait()
     t_mate.wait()
     head_swap.wait_send()
@@ -429,10 +440,12 @@
             dma((2, 7)),
             dma((5, 4)),
             dma((5, 4)),
-            dma((3,)),
-            dma((3,)),
-            dma((9,)),
-            dma((9,)),
+            dma((2,)),
+            dma((2,)),
+            dma((8,)),
+            dma((8,)),
+            dma((10,)),
+            dma((10,)),
             dma((3, 4)),
             dma((3, 4)),
             dma((2, 20)),

time: 207 us -> 142 us (0.69)
  Pallas kernels: 206 us -> 141 us
    pallas_call x1, Pallas kernels: 168 us -> 103 us  [reduce_all(): pl.pallas_call(reduce_kernel, in_specs=[hbm, hbm, hbm, vmem, hbm, hbm, hb...]
where the time goes in v3:
time: 142 us; the launch traced here: 141 us
  Pallas kernels  141 us (99%)
    pallas_call x1, Pallas kernels, reduce_all(): pl.pallas_call(reduce_kernel, in_specs=[hbm, hbm, hbm, vmem, hbm, hbm, hb...  103 us
    pallas_call x1, Pallas kernels, queries(): pl.pallas_call(query_kernel, grid_spec=pltpu.PrefetchScalarGridSpec(num_s...  38 us

profile of v3, /device:TPU:1, one launch (start us, length us, event | category | flops | bytes accessed | tf_op | source)
XLA Modules:
  0.0 141.5 jit_solution(16788183253815227790)
XLA Ops:
  0.6 102.8 %reduce_all.1 = (bf16[4,2048,640]{2,1,0:T(8,128)(2,1)}, bf16[1024,1280]{1,0:T(8,128)(2,1)}, bf16[4,4,2,2,40,1280]{5,4,3,2,1,0:T(8,128)(2,1)}, f32[2,8,640]{2,1,0:T(8,128)}, f32[2,8,640]{2,1,0:T(8,128)}) custom-call(bf16[1024,1280]{1,0:T(8,128)(2,1)} %k_hbm.1, bf16[1024,1280]{1,0:T(8,128)(2,1)} %v_hbm.1, bf16[1024,1280]{1,0:T(8,128)(2,1)} %q_ref.1, ...), custom_call_target="tpu_custom_call" | custom-call | tf_op jit(solution)/shard_map/reduce_all/pallas_call | solution.py:418
  103.4 38.0 %queries.1 = (bf16[1024,1280]{1,0:T(8,128)(2,1)}, bf16[2,640,640]{2,1,0:T(8,128)(2,1)}, bf16[2,640,640]{2,1,0:T(8,128)(2,1)}, bf16[2,640,640]{2,1,0:T(8,128)(2,1)}) custom-call(s32[1]{0:T(128)} %bitcast.meta, bf16[1024,1280]{1,0:T(8,128)(2,1)} %q_ref.1, bf16[1024,1280]{1,0:T(8,128)(2,1)} %get-tuple-element.9.x_ref, ...), custom_call_target="tpu_custom_call" | custom-call | tf_op jit(solution)/shard_map/queries/pallas_call | solution.py:534

commit v4 on v3

--- a/solution.py
+++ b/solution.py
@@ -72,12 +72,27 @@
     return pl.ds(pl.multiple_of(start, align), size)
 
 
+def renormed(moved, sum_w):
+    moved = moved.astype(F32)
+    scale = jnp.sqrt(sum_w + 1e-06) / jnp.sqrt(jnp.sum(moved * moved, axis=0, keepdims=True) + 1e-06)
+    return (moved * scale).astype(BF16)
+
+
+def apply_head(q, w_cat, w_out, gain):
+    pre = dot(q, w_cat, ((1,), (0,)))
+    pre_in = pre[:, :W]
+    hidden = (pre_in * jax.nn.sigmoid(pre_in) * pre[:, W:]).astype(BF16)
+    head_out = dot(hidden, w_out, ((1,), (0,)))
+    inverse = lax.rsqrt(jnp.mean(head_out * head_out, axis=-1, keepdims=True) + 1e-06)
+    return (head_out * inverse * gain).astype(BF16)
+
+
 def reduce_kernel(
     k_hbm, v_hbm, q_hbm, lr_ref, wi_hbm, wg_hbm, wo_hbm, gain_ref, proj_hbm,
-    u_ref, q_out, t_ref, aux_ref, auxo_ref,
-    kbuf, vbuf, wcat, wout, acc, send, core_buf, s0, s1, s2, s3, s4, r0, r1, r2, r3, r4, shard,
+    u_ref, q_out, t_ref, normed_ref, ni_ref, ng_ref, no_ref, aux_ref, auxo_ref,
+    kbuf, vbuf, wcat, wout, acc, send, core_buf, s0, s1, s2, s3, s4, r0, r1, r2, r3, r4, shard, u_own,
     ld_sem, s_sem, r_sem, m_ssem, m_rsem, q_ssem, q_rsem, t_ssem, t_rsem, f_ssem, f_rsem, g_ssem, g_rsem,
-    fw_ssem, fw_rsem, l_sem,
+    fw_ssem, fw_rsem, l_sem, o_sem,
 ):
     z, y, x_hi, core, x_lo = position()
     bits = bits_of(z, y)
@@ -261,6 +276,13 @@
 
     lax.fori_loop(0, 4, tile_step, 0)
 
+    q_loads = []
+    for i in range(2):
+        h = 1 - core if i == 0 else core
+        cols = pl.ds(pl.multiple_of(h * W, 128), W)
+        q_loads.append(pltpu.make_async_copy(q_hbm.at[:, cols], kbuf.at[i], ld_sem.at[i, 0]))
+        q_loads[-1].start()
+
     finals = final_rows()
     for p in range(4):
         for n in range(3):
@@ -331,77 +353,164 @@
             by_core(t_three, lambda copy: copy.wait())
             t_mate.start()
 
-    own, other = 2 * x_lo + core, 2 * (1 - x_lo) + core
-    locals_, firsts = [], []
+    firsts = []
     for p in range(4):
         copies[4][p].wait_recv()
-        shard[p, :, :] = (acc[rows(base[p], 16), :] + r4[p, :, :].astype(F32)).astype(BF16)
-        dst = u_ref.at[own, rows(base[p], 16)]
+        at = rows(base[p], 16)
+        block = (acc[at, :] + r4[p, :, :].astype(F32)).astype(BF16)
+        shard[p, :, :] = block
+        u_own[1, at, :] = block
+        dsts = u_own.at[1, at], u_ref.at[core, at], u_ref.at[core, at]
         for n, dev in enumerate((far, side, cross)):
-            copy = remote(shard.at[p], dst, f_ssem.at[n, p], f_rsem.at[n, p], dev)
+            copy = remote(shard.at[p], dsts[n], f_ssem.at[n, p], f_rsem.at[n, p], dev)
             copy.start()
             firsts.append(copy)
-        local = pltpu.make_async_copy(shard.at[p], dst, l_sem.at[1 + p])
-        local.start()
-        locals_.append(local)
-        base[p] = base[p] - x_hi * 16
-    for copy in locals_:
+
+    known = {3: [base[p] - x_hi * 16 for p in range(4)]}
+    for step in (3, 2, 1):
+        known[step - 1] = [
+            known[step][p] - bits[(p + step) % 4] * (256 >> step) for p in range(4)
+        ]
+    own_copies, other_copies, forwards = {}, {}, []
+
+    def start_own(step):
+        size = 256 >> step
+        own_copies[step] = []
+        for p in range(4):
+            block = u_own.at[1, rows(known[step][p], size, min(size, 32))]
+            sem = (0, 4 * step + p)
+            copy = remote(block, block, g_ssem.at[sem], g_rsem.at[sem], peers[(p + step) % 4])
+            copy.start()
+            own_copies[step].append(copy)
+
+    def other_step(step):
+        parts = 2 if step == 0 else 1
+        size = (256 >> step) // parts
+        out = []
+        for c in range(parts):
+            for p in range(4):
+                block = u_ref.at[core, rows(known[step][p] + c * size, size, 32)]
+                sem = (1, 16 * c + 4 * step + p)
+                out.append(
+                    remote(block, block, g_ssem.at[sem], g_rsem.at[sem], peers[(p + step) % 4])
+                )
+        other_copies[step] = out
+
+    def wait_all(copies):
+        for copy in copies:
+            copy.wait_recv()
+
+    def start_all(copies):
+        for copy in copies:
+            copy.start()
+
+    def forward(src_of, dst_of, at, size):
+        n = len(forwards)
+        where = rows(at, size, 32)
+        copy = remote(src_of(where), dst_of(where), fw_ssem.at[n], fw_rsem.at[n], mate)
+        forwards.append(copy)
+        return copy
+
+    def own_forward(at, size):
+        return forward(lambda w: u_own.at[1, w], lambda w: u_own.at[0, w], at, size)
+
+    def other_forward(at, size):
+        return forward(lambda w: u_ref.at[core, w], lambda w: u_ref.at[core, w], at, size)
+
+    theirs = [known[0][p] + (1 - 2 * bits[p]) * 256 for p in range(4)]
+    for step in range(4):
+        other_step(step)
+    wait_all(firsts[0::3])
+    start_own(3)
+    wait_all(firsts[1::3])
+    wait_all(firsts[2::3])
+    start_all(other_copies[3])
+    start_all(q_copies[5:])
+    for step in (2, 1):
+        wait_all(own_copies[step + 1])
+        start_own(step)
+        wait_all(other_copies[step + 1])
+        start_all(other_copies[step])
+    wait_all(own_copies[1])
+    start_own(0)
+    own_fw = [own_forward(known[0][p], 256) for p in range(4)]
+    start_all(own_fw)
+    late_fw = [own_forward(theirs[p], 256) for p in range(4)]
+    for p in range(4):
+        own_copies[0][p].wait_recv()
+        late_fw[p].start()
+    early_fw = [other_forward(known[0][p], 256) for p in range(4)]
+    last_fw = [other_forward(theirs[p] + c * 128, 128) for c in range(2) for p in range(4)]
+
+    for copy in q_loads:
         copy.wait()
-    for copy in firsts:
-        copy.wait_recv()
-    for copy in q_copies[5:]:
-        copy.start()
-    gathers, forwards = [], []
-    waiting = [[] for _ in range(4)]
-    size = 32
-    for step in range(3, -1, -1):
-        parts = 2 if step == 0 else 1
-        piece = size // parts
-        arrived = [list(w) for w in waiting]
-        waiting = [[] for _ in range(4)]
-        for p in range(4):
-            for copy in arrived[p]:
-                copy.wait_recv()
-        for g, head in enumerate((own, other)):
-            for c in range(parts):
-                for p in range(4):
-                    d = (p + step) % 4
-                    block = u_ref.at[head, rows(base[p] + c * piece, piece, 32)]
-                    sem = (g, 4 * (step + c) + p) if step == 0 else (g, 4 * (step + 1) + p)
-                    copy = remote(block, block, g_ssem.at[sem], g_rsem.at[sem], peers[d])
-                    copy.start()
-                    gathers.append(copy)
-                    waiting[p].append(copy)
-        if step == 0:
-            n = 0
-            for head in (own, other):
-                for p in range(4):
-                    block = u_ref.at[head, rows(base[p], size, 32)]
-                    copy = remote(block, block, fw_ssem.at[n], fw_rsem.at[n], mate)
-                    copy.start()
-                    forwards.append(copy)
-                    n += 1
-            for g, head in enumerate((own, other)):
-                for c in range(2):
-                    for p in range(4):
-                        waiting[p][2 * g + c].wait_recv()
-                        theirs = base[p] + (1 - 2 * bits[p]) * size
-                        block = u_ref.at[head, rows(theirs + c * piece, piece, 32)]
-                        copy = remote(block, block, fw_ssem.at[n], fw_rsem.at[n], mate)
-                        copy.start()
-                        forwards.append(copy)
-                        n += 1
-        for p in range(4):
-            base[p] = base[p] - bits[(p + step) % 4] * size
-        size *= 2
-    for copy in forwards:
-        copy.wait_recv()
+
+    def new_weights(i, h):
+        return (
+            pltpu.make_async_copy(wcat.at[i, :, pl.ds(0, W)], ni_ref.at[h], o_sem.at[i, 0]),
+            pltpu.make_async_copy(wcat.at[i, :, pl.ds(W, W)], ng_ref.at[h], o_sem.at[i, 1]),
+            pltpu.make_async_copy(wout.at[i], no_ref.at[h], o_sem.at[i, 2]),
+        )
+
+    def normed_out(i, h):
+        cols = pl.ds(pl.multiple_of(h * W, 128), W)
+        return pltpu.make_async_copy(vbuf.at[i], normed_ref.at[:, cols], o_sem.at[i, 3])
+
+    def query_step(n, carry):
+        i, t = 1 - n // 2, n % 2
+        h = jnp.where(i == 0, 1 - core, core)
+
+        @pl.when(n == 2)
+        def _():
+            wait_all(own_fw)
+            wait_all(late_fw)
+
+        @pl.when(t == 0)
+        def _():
+            for m in range(3):
+                fresh = renormed(u_own[i, m * W : (m + 1) * W, :], aux_ref[h, m : m + 1, :])
+                if m < 2:
+                    wcat[i, :, m * W : (m + 1) * W] = fresh
+                else:
+                    wout[i] = fresh
+            for copy in new_weights(i, h):
+                copy.start()
+
+        at = rows(t * TM, TM, TM)
+        vbuf[i, at, :] = apply_head(kbuf[i, at, :], wcat[i], wout[i], aux_ref[h, 3:4, :])
+
+        @pl.when(n == 0)
+        def _():
+            wait_all(other_copies[1])
+            start_all(other_copies[0])
+            start_all(early_fw)
+
+        @pl.when(t == 1)
+        def _():
+            normed_out(i, h).start()
+
+        return carry
+
+    lax.fori_loop(0, 4, query_step, 0)
+
+    for n in range(8):
+        other_copies[0][n].wait_recv()
+        last_fw[n].start()
+    wait_all(early_fw)
+    wait_all(last_fw)
     for copy in q_copies:
         copy.wait()
     aux_copy.wait()
     t_mate.wait()
     head_swap.wait_send()
-    for copy in (*forwards, *gathers, *firsts):
+    for i in range(2):
+        h = 1 - core if i == 0 else core
+        for copy in (*new_weights(i, h), normed_out(i, h)):
+            copy.wait()
+    for step in range(4):
+        for copy in (*own_copies[step], *other_copies[step]):
+            copy.wait_send()
+    for copy in (*forwards, *firsts):
         copy.wait_send()
     for step in range(5):
         for p in range(4):
@@ -418,11 +527,15 @@
     return pl.pallas_call(
         reduce_kernel,
         in_specs=[hbm, hbm, hbm, vmem, hbm, hbm, hbm, vmem, hbm],
-        out_specs=[hbm, hbm, hbm, vmem, vmem],
+        out_specs=[hbm, hbm, hbm, hbm, hbm, hbm, hbm, vmem, vmem],
         out_shape=[
-            jax.ShapeDtypeStruct((4, R, W), BF16),
+            jax.ShapeDtypeStruct((2, R, W), BF16),
             jax.ShapeDtypeStruct(q.shape, BF16),
             jax.ShapeDtypeStruct((4, 4, 2, 2, *proj.shape), BF16),
+            jax.ShapeDtypeStruct(q.shape, BF16),
+            jax.ShapeDtypeStruct((2, W, W), BF16),
+            jax.ShapeDtypeStruct((2, W, W), BF16),
+            jax.ShapeDtypeStruct((2, W, W), BF16),
             jax.ShapeDtypeStruct((2, 8, W), F32),
             jax.ShapeDtypeStruct((2, 8, W), F32),
         ],
@@ -437,6 +550,7 @@
             *bufs,
             *bufs,
             pltpu.VMEM((4, 16, W), BF16),
+            pltpu.VMEM((2, R, W), BF16),
             dma((2, 7)),
             dma((5, 4)),
             dma((5, 4)),
@@ -450,9 +564,10 @@
             dma((3, 4)),
             dma((2, 20)),
             dma((2, 20)),
-            dma((24,)),
-            dma((24,)),
-            dma((5,)),
+            dma((20,)),
+            dma((20,)),
+            dma((1,)),
+            dma((2, 4)),
         ],
         compiler_params=pltpu.CompilerParams(
             collective_id=0, has_side_effects=True, vmem_limit_bytes=VMEM_LIMIT
@@ -462,125 +577,102 @@
 
 
 def query_kernel(
-    meta, q_ref, x_ref, ui_ref, ug_ref, uo_ref, aux_ref, auxo_ref, proj_ref,
-    out_ref, ni_ref, ng_ref, no_ref, wcat, wout, total,
+    normed_hbm, q_hbm, u_hbm, aux_ref, t_hbm, ni_hbm, ng_hbm, no_hbm,
+    out_hbm, ni_out, ng_out, no_out,
+    nbuf, qbuf, ubuf, tbuf, wbuf, wcat, wout, xbuf, obuf, in_sem, out_sem,
 ):
-    j, t = pl.program_id(0), pl.program_id(1)
-    mine = j < 2
-    aux = jnp.where(mine, aux_ref[...], auxo_ref[...])
-
-    @pl.when(t == 0)
-    def _():
-        for n, ref in enumerate((ui_ref, ug_ref, uo_ref)):
-            moved = ref[...].astype(F32)
-            scale = jnp.sqrt(aux[n : n + 1, :] + 1e-06) / jnp.sqrt(
-                jnp.sum(moved * moved, axis=0, keepdims=True) + 1e-06
+    x_lo = lax.axis_index("head")
+    load = pltpu.make_async_copy
+    heads = []
+    for h in range(2):
+        cols = pl.ds(h * W, W)
+        heads.append(
+            (
+                load(u_hbm.at[h, pl.ds(0, 3 * W)], ubuf.at[h], in_sem.at[0, h]),
+                load(q_hbm.at[:, cols], qbuf.at[h], in_sem.at[1, h]),
             )
-            fresh = (moved * scale).astype(BF16)
-            if n < 2:
-                wcat[:, n * W : (n + 1) * W] = fresh
+        )
+    own_side = load(normed_hbm, nbuf, in_sem.at[2, 0])
+    t_own = load(t_hbm.at[x_lo], tbuf.at[0], in_sem.at[2, 1])
+    t_other = load(t_hbm.at[1 - x_lo], tbuf.at[1], in_sem.at[3, 0])
+    new = (ni_hbm, ng_hbm, no_hbm), (ni_out, ng_out, no_out)
+    through = [
+        (load(new[0][n], wbuf.at[n], in_sem.at[4 + n, 0]), load(wbuf.at[n], new[1][n], in_sem.at[4 + n, 1]))
+        for n in range(3)
+    ]
+    for copy in (*heads[0], *heads[1], own_side, t_own, t_other, *(pair[0] for pair in through)):
+        copy.start()
+    tok = nbuf.shape[0]
+    for h in range(2):
+        for copy in heads[h]:
+            copy.wait()
+        for m in range(3):
+            fresh = renormed(ubuf[h, m * W : (m + 1) * W, :], aux_ref[h, m : m + 1, :])
+            if m < 2:
+                wcat[h, :, m * W : (m + 1) * W] = fresh
             else:
-                wout[...] = fresh
-
-        @pl.when(mine)
-        def _():
-            ni_ref[...] = wcat[:, :W]
-            ng_ref[...] = wcat[:, W:]
-            no_ref[...] = wout[...]
-
-    q = jnp.where(mine, q_ref[...], x_ref[...])
-    pre = dot(q, wcat[...], ((1,), (0,)))
-    pre_in = pre[:, :W]
-    hidden = (pre_in * jax.nn.sigmoid(pre_in) * pre[:, W:]).astype(BF16)
-    head_out = dot(hidden, wout[...], ((1,), (0,)))
-    inverse = lax.rsqrt(jnp.mean(head_out * head_out, axis=-1, keepdims=True) + 1e-06)
-    normed = (head_out * inverse * aux[3:4, :]).astype(BF16)
-    part = dot(normed, proj_ref[...], ((1,), (1,)))
-    tm = part.shape[0]
-    at = pl.ds(pl.multiple_of(t * tm, tm), tm)
-
-    @pl.when(j == 0)
-    def _():
-        total[at, :] = part
-
-    @pl.when((j > 0) & (j < 3))
-    def _():
-        total[at, :] += part
-
-    @pl.when(j == 3)
-    def _():
-        out_ref[...] = (total[at, :] + part).astype(BF16)
-
-
-def queries(meta, q, x, u, aux, auxo, proj, tm=1024):
-    tok = q.shape[0]
-    steps = tok // tm
+                wout[h] = fresh
+        xbuf[:, h * W : (h + 1) * W] = apply_head(qbuf[h], wcat[h], wout[h], aux_ref[h, 3:4, :])
+    for pair in through:
+        pair[0].wait()
+        pair[1].start()
+    for copy in (own_side, t_own, t_other):
+        copy.wait()
+    outs = []
+    for t in range(tok // TM):
+        at = pl.ds(t * TM, TM)
+        obuf[at, :] = (
+            dot(nbuf[at, :], tbuf[0], ((1,), (1,))) + dot(xbuf[at, :], tbuf[1], ((1,), (1,)))
+        ).astype(BF16)
+        outs.append(load(obuf.at[at], out_hbm.at[at], out_sem.at[t]))
+        outs[-1].start()
+    for copy in (*outs, *(pair[1] for pair in through)):
+        copy.wait()
+
+
+def queries(normed, q, u, aux, proj, ni, ng, no):
+    tok, width = q.shape
     feat = proj.shape[1]
-
-    def head(j, m):
-        own = j < 2
-        return jnp.where(own, 2 * m[0] + j, 2 * (1 - m[0]) + j - 2)
-
-    def q_map(j, t, m):
-        return jnp.where(j < 2, t, steps - 1), jnp.minimum(j, 1)
-
-    def x_map(j, t, m):
-        return jnp.where(j < 2, 0, t), jnp.maximum(j - 2, 0)
-
-    def weight(n):
-        return pl.BlockSpec((None, W, W), lambda j, t, m: (head(j, m), n, 0))
-
-    new = pl.BlockSpec((None, W, W), lambda j, t, m: (jnp.minimum(j, 1), 0, 0))
+    hbm = pl.BlockSpec(memory_space=pl.ANY)
+    vmem = pl.BlockSpec(memory_space=pltpu.VMEM)
+    dma = pltpu.SemaphoreType.DMA
     return pl.pallas_call(
         query_kernel,
-        grid_spec=pltpu.PrefetchScalarGridSpec(
-            num_scalar_prefetch=1,
-            grid=(4, steps),
-            in_specs=[
-                pl.BlockSpec((tm, W), q_map),
-                pl.BlockSpec((tm, W), x_map),
-                weight(0),
-                weight(1),
-                weight(2),
-                pl.BlockSpec((None, 8, W), lambda j, t, m: (jnp.minimum(j, 1), 0, 0)),
-                pl.BlockSpec((None, 8, W), lambda j, t, m: (jnp.maximum(j - 2, 0), 0, 0)),
-                pl.BlockSpec(
-                    (None, feat, W), lambda j, t, m: (head(j, m) // 2, 0, head(j, m) % 2)
-                ),
-            ],
-            out_specs=[
-                pl.BlockSpec((tm, feat), lambda j, t, m: (jnp.where(j == 3, t, 0), 0)),
-                new,
-                new,
-                new,
-            ],
-            scratch_shapes=[
-                pltpu.VMEM((W, 2 * W), BF16),
-                pltpu.VMEM((W, W), BF16),
-                pltpu.VMEM((tok, feat), F32),
-            ],
-        ),
+        in_specs=[hbm, hbm, hbm, vmem, hbm, hbm, hbm, hbm],
+        out_specs=[hbm] * 4,
         out_shape=[
             jax.ShapeDtypeStruct((tok, feat), BF16),
-            jax.ShapeDtypeStruct((2, W, W), BF16),
-            jax.ShapeDtypeStruct((2, W, W), BF16),
-            jax.ShapeDtypeStruct((2, W, W), BF16),
+            jax.ShapeDtypeStruct(ni.shape, BF16),
+            jax.ShapeDtypeStruct(ng.shape, BF16),
+            jax.ShapeDtypeStruct(no.shape, BF16),
+        ],
+        scratch_shapes=[
+            pltpu.VMEM((tok, width), BF16),
+            pltpu.VMEM((2, tok, W), BF16),
+            pltpu.VMEM((2, 3 * W, W), BF16),
+            pltpu.VMEM((2, feat, width), BF16),
+            pltpu.VMEM((3, *ni.shape), BF16),
+            pltpu.VMEM((2, W, 2 * W), BF16),
+            pltpu.VMEM((2, W, W), BF16),
+            pltpu.VMEM((tok, width), BF16),
+            pltpu.VMEM((tok, feat), BF16),
+            dma((7, 2)),
+            dma((tok // TM,)),
         ],
         compiler_params=pltpu.CompilerParams(vmem_limit_bytes=VMEM_LIMIT),
         name="queries",
-    )(meta, q, x, u, u, u, aux, auxo, proj)
+    )(normed, q, u, aux, proj, ni, ng, no)
 
 
 def on_device(
     key_rows, value_rows, query_rows, learn_rates, fast_in, fast_gate, fast_out, head_gain, out_proj
 ):
-    u, swapped, proj, aux, auxo = reduce_all(
+    u, swapped, proj, normed, ni, ng, no, _, auxo = reduce_all(
         key_rows, value_rows, query_rows, learn_rates, fast_in, fast_gate, fast_out, head_gain,
         out_proj.T,
     )
     proj = proj.reshape(2, -1, proj.shape[-1])
-    x_lo = lax.axis_index("head").reshape(1).astype(jnp.int32)
-    return tuple(queries(x_lo, query_rows, swapped, u, aux, auxo, proj))
+    return tuple(queries(normed, swapped, u, auxo, proj, ni, ng, no))
 
 
 def solution(mesh):

time: 142 us -> 127 us (0.89)
  Pallas kernels: 141 us -> 126 us
    pallas_call x1, Pallas kernels: 38 us -> 20.4 us  [queries(): pl.pallas_call(query_kernel, in_specs=[hbm, hbm, hbm, vmem, hbm, hbm, hbm...]
    pallas_call x1, Pallas kernels: 103 us -> 105 us  [reduce_all(): pl.pallas_call(reduce_kernel, in_specs=[hbm, hbm, hbm, vmem, hbm, hbm, hb...]
where the time goes in v4:
time: 127 us
  Pallas kernels  126 us (99%)
    pallas_call x1, Pallas kernels, reduce_all(): pl.pallas_call(reduce_kernel, in_specs=[hbm, hbm, hbm, vmem, hbm, hbm, hb...  105 us
    pallas_call x1, Pallas kernels, queries(): pl.pallas_call(query_kernel, in_specs=[hbm, hbm, hbm, vmem, hbm, hbm, hbm...  20.4 us

profile of v4, /device:TPU:1, one launch (start us, length us, event | category | flops | bytes accessed | tf_op | source)
XLA Modules:
  0.0 126.6 jit_solution(4605120985112480257)
XLA Ops:
  0.6 105.4 %reduce_all.1 = (bf16[2,2048,640]{2,1,0:T(8,128)(2,1)}, bf16[1024,1280]{1,0:T(8,128)(2,1)}, bf16[4,4,2,2,40,1280]{5,4,3,2,1,0:T(8,128)(2,1)}, bf16[1024,1280]{1,...) custom-call(bf16[1024,1280]{1,0:T(8,128)(2,1)} %k_hbm.1, ...), custom_call_target="tpu_custom_call" | custom-call | tf_op jit(solution)/shard_map/reduce_all/pallas_call | solution.py:527
  106.1 20.4 %queries.1 = (bf16[1024,1280]{1,0:T(8,128)(2,1)}, bf16[2,640,640]{2,1,0:T(8,128)(2,1)}, bf16[2,640,640]{2,1,0:T(8,128)(2,1)}, bf16[2,640,640]{2,1,0:T(8,128)(2,1)}) custom-call(bf16[1024,1280]{1,0:T(8,128)(2,1)} %get-tuple-element.12.normed_hbm, bf16[1024,1280]{1,0:T(8,128)(2,1)} %get-tuple-element.13.q_hbm, bf16[2,2048,640]{2,1,0:T(8,128)(2,1)} %get-tuple-element.14.u_hbm, ...), custom_call_target="tpu_custom_call" | custom-call | tf_op jit(solution)/shard_map/queries/pallas_call | solution.py:639

commit v5 on v4

--- a/solution.py
+++ b/solution.py
@@ -306,24 +306,40 @@
             out_at = base[p] + (1 - bit) * half
             kept_at[p] = base[p] + bit * half
             if step > 0:
-                copies[step - 1][p].wait_recv()
+                copies[step - 1][p][0].wait_recv()
             got_ref = core_buf if step == 0 else rbuf[step - 1].at[p]
             got_at = out_at if step == 0 else (1 - bit) * half
-            into = sbuf[step].at[p]
-
-            def emit(o, size, out_at=out_at, got_at=got_at, into=into, got_ref=got_ref):
-                into[rows(o, size), :] = (
-                    acc[rows(out_at + o, size), :] + got_ref[rows(got_at + o, size), :].astype(F32)
-                ).astype(BF16)
-
-            rows_loop(half, emit)
-            copies[step][p] = remote(
-                sbuf[step].at[p], rbuf[step].at[p], s_sem.at[step, p], r_sem.at[step, p],
-                peers[d] if step < 4 else far,
-            )
-            copies[step][p].start()
+            into, landing = sbuf[step].at[p], rbuf[step].at[p]
+            if step < 4:
+                next_bit = bits[(p + step + 1) % 4] if step < 3 else x_hi
+                size = half // 2
+                offsets = (1 - next_bit) * size, next_bit * size
+            else:
+                size, offsets = half, (0,)
+            copies[step][p] = []
+            for n, off in enumerate(offsets):
+
+                def emit(
+                    o, count, out_at=out_at + off, got_at=got_at + off, into_at=off,
+                    into=into, got_ref=got_ref,
+                ):
+                    into[rows(into_at + o, count), :] = (
+                        acc[rows(out_at + o, count), :]
+                        + got_ref[rows(got_at + o, count), :].astype(F32)
+                    ).astype(BF16)
+
+                rows_loop(size, emit)
+                piece = rows(off, size)
+                copy = remote(
+                    into.at[piece], landing.at[piece], s_sem.at[step, p, n], r_sem.at[step, p, n],
+                    peers[d] if step < 4 else far,
+                )
+                copy.start()
+                copies[step][p].append(copy)
         for p in range(4):
             bit = bits[(p + step) % 4] if step < 4 else x_hi
+            if step > 0:
+                copies[step - 1][p][1].wait_recv()
             got_ref = core_buf if step == 0 else rbuf[step - 1].at[p]
             got_at = kept_at[p] if step == 0 else bit * half
 
@@ -355,7 +371,7 @@
 
     firsts = []
     for p in range(4):
-        copies[4][p].wait_recv()
+        copies[4][p][0].wait_recv()
         at = rows(base[p], 16)
         block = (acc[at, :] + r4[p, :, :].astype(F32)).astype(BF16)
         shard[p, :, :] = block
@@ -371,30 +387,12 @@
         known[step - 1] = [
             known[step][p] - bits[(p + step) % 4] * (256 >> step) for p in range(4)
         ]
-    own_copies, other_copies, forwards = {}, {}, []
-
-    def start_own(step):
-        size = 256 >> step
-        own_copies[step] = []
-        for p in range(4):
-            block = u_own.at[1, rows(known[step][p], size, min(size, 32))]
-            sem = (0, 4 * step + p)
-            copy = remote(block, block, g_ssem.at[sem], g_rsem.at[sem], peers[(p + step) % 4])
-            copy.start()
-            own_copies[step].append(copy)
-
-    def other_step(step):
-        parts = 2 if step == 0 else 1
-        size = (256 >> step) // parts
-        out = []
-        for c in range(parts):
-            for p in range(4):
-                block = u_ref.at[core, rows(known[step][p] + c * size, size, 32)]
-                sem = (1, 16 * c + 4 * step + p)
-                out.append(
-                    remote(block, block, g_ssem.at[sem], g_rsem.at[sem], peers[(p + step) % 4])
-                )
-        other_copies[step] = out
+    theirs = {
+        step: [known[step][p] + (1 - 2 * bits[(p + step) % 4]) * (256 >> step) for p in range(4)]
+        for step in range(4)
+    }
+    shard_far = [base[p] + (1 - 2 * x_hi) * 16 for p in range(4)]
+    forwards, exchanged = [], []
 
     def wait_all(copies):
         for copy in copies:
@@ -404,43 +402,78 @@
         for copy in copies:
             copy.start()
 
-    def forward(src_of, dst_of, at, size):
+    def exchange(g, step, piece, starts, size):
+        out = []
+        for p in range(4):
+            ref = u_own.at[1] if g == 0 else u_ref.at[core]
+            block = ref.at[rows(starts[p], size)]
+            sem = (g, 8 * step + 4 * piece + p)
+            out.append(remote(block, block, g_ssem.at[sem], g_rsem.at[sem], peers[(p + step) % 4]))
+        exchanged.extend(out)
+        return out
+
+    own_a = {3: exchange(0, 3, 0, base, 16)}
+    own_b = {3: exchange(0, 3, 1, shard_far, 16)}
+    other_a = {}
+    other_b = {3: exchange(1, 3, 1, known[3], 32)}
+    for step in (2, 1, 0):
+        size = 256 >> (step + 1)
+        own_a[step] = exchange(0, step, 0, known[step + 1], size)
+        own_b[step] = exchange(0, step, 1, theirs[step + 1], size)
+        other_a[step] = exchange(1, step, 0, known[step + 1], size)
+        other_b[step] = exchange(1, step, 1, theirs[step + 1], size)
+
+    def wait_own(step):
+        wait_all(own_a[step])
+        wait_all(own_b[step])
+
+    def wait_other(step):
+        if step < 3:
+            wait_all(other_a[step])
+        wait_all(other_b[step])
+
+    def forward(g, at, size):
         n = len(forwards)
-        where = rows(at, size, 32)
-        copy = remote(src_of(where), dst_of(where), fw_ssem.at[n], fw_rsem.at[n], mate)
+        where = rows(at, size)
+        src = u_own.at[1, where] if g == 0 else u_ref.at[core, where]
+        dst = u_own.at[0, where] if g == 0 else u_ref.at[core, where]
+        copy = remote(src, dst, fw_ssem.at[n], fw_rsem.at[n], mate)
         forwards.append(copy)
         return copy
 
-    def own_forward(at, size):
-        return forward(lambda w: u_own.at[1, w], lambda w: u_own.at[0, w], at, size)
-
-    def other_forward(at, size):
-        return forward(lambda w: u_ref.at[core, w], lambda w: u_ref.at[core, w], at, size)
-
-    theirs = [known[0][p] + (1 - 2 * bits[p]) * 256 for p in range(4)]
-    for step in range(4):
-        other_step(step)
+    own_fw = [forward(0, known[0][p], 256) for p in range(4)]
+    late_fw = [forward(0, theirs[0][p], 256) for p in range(4)]
+    other_fw = [forward(1, known[0][p], 256) for p in range(4)]
+    last_fw = [forward(1, theirs[0][p], 256) for p in range(4)]
+
+    start_all(own_a[3])
     wait_all(firsts[0::3])
-    start_own(3)
+    start_all(own_b[3])
+    start_all(own_a[2])
     wait_all(firsts[1::3])
     wait_all(firsts[2::3])
-    start_all(other_copies[3])
+    start_all(other_b[3])
+    start_all(other_a[2])
     start_all(q_copies[5:])
-    for step in (2, 1):
-        wait_all(own_copies[step + 1])
-        start_own(step)
-        wait_all(other_copies[step + 1])
-        start_all(other_copies[step])
-    wait_all(own_copies[1])
-    start_own(0)
-    own_fw = [own_forward(known[0][p], 256) for p in range(4)]
+    wait_own(3)
+    start_all(own_b[2])
+    start_all(own_a[1])
+    wait_other(3)
+    start_all(other_b[2])
+    start_all(other_a[1])
+    wait_own(2)
+    start_all(own_b[1])
+    start_all(own_a[0])
+    wait_other(2)
+    start_all(other_b[1])
+    wait_own(1)
+    start_all(own_b[0])
     start_all(own_fw)
-    late_fw = [own_forward(theirs[p], 256) for p in range(4)]
+    start_all(other_a[0])
     for p in range(4):
-        own_copies[0][p].wait_recv()
+        own_a[0][p].wait_recv()
+        own_b[0][p].wait_recv()
         late_fw[p].start()
-    early_fw = [other_forward(known[0][p], 256) for p in range(4)]
-    last_fw = [other_forward(theirs[p] + c * 128, 128) for c in range(2) for p in range(4)]
 
     for copy in q_loads:
         copy.wait()
@@ -481,9 +514,16 @@
 
         @pl.when(n == 0)
         def _():
-            wait_all(other_copies[1])
-            start_all(other_copies[0])
-            start_all(early_fw)
+            wait_other(1)
+            start_all(other_b[0])
+            start_all(other_fw)
+
+        @pl.when(n == 2)
+        def _():
+            for p in range(4):
+                other_a[0][p].wait_recv()
+                other_b[0][p].wait_recv()
+                last_fw[p].start()
 
         @pl.when(t == 1)
         def _():
@@ -493,10 +533,7 @@
 
     lax.fori_loop(0, 4, query_step, 0)
 
-    for n in range(8):
-        other_copies[0][n].wait_recv()
-        last_fw[n].start()
-    wait_all(early_fw)
+    wait_all(other_fw)
     wait_all(last_fw)
     for copy in q_copies:
         copy.wait()
@@ -507,14 +544,12 @@
         h = 1 - core if i == 0 else core
         for copy in (*new_weights(i, h), normed_out(i, h)):
             copy.wait()
-    for step in range(4):
-        for copy in (*own_copies[step], *other_copies[step]):
-            copy.wait_send()
-    for copy in (*forwards, *firsts):
+    for copy in (*exchanged, *forwards, *firsts):
         copy.wait_send()
     for step in range(5):
         for p in range(4):
-            copies[step][p].wait_send()
+            for copy in copies[step][p]:
+                copy.wait_send()
 
 
 def reduce_all(k, v, q, lr, wi, wg, wo, gain, proj):
@@ -552,8 +587,8 @@
             pltpu.VMEM((4, 16, W), BF16),
             pltpu.VMEM((2, R, W), BF16),
             dma((2, 7)),
-            dma((5, 4)),
-            dma((5, 4)),
+            dma((5, 4, 2)),
+            dma((5, 4, 2)),
             dma((2,)),
             dma((2,)),
             dma((8,)),
@@ -562,10 +597,10 @@
             dma((10,)),
             dma((3, 4)),
             dma((3, 4)),
-            dma((2, 20)),
-            dma((2, 20)),
-            dma((20,)),
-            dma((20,)),
+            dma((2, 32)),
+            dma((2, 32)),
+            dma((16,)),
+            dma((16,)),
             dma((1,)),
             dma((2, 4)),
         ],

time: 127 us -> 123 us (0.969)
  Pallas kernels: 126 us -> 122 us
    pallas_call x1, Pallas kernels: 105 us -> 102 us  [reduce_all(): pl.pallas_call(reduce_kernel, in_specs=[hbm, hbm, hbm, vmem, hbm, hbm, hb...]
where the time goes in v5:
time: 123 us
  Pallas kernels  122 us (99%)
    pallas_call x1, Pallas kernels, reduce_all(): pl.pallas_call(reduce_kernel, in_specs=[hbm, hbm, hbm, vmem, hbm, hbm, hb...  102 us
    pallas_call x1, Pallas kernels, queries(): pl.pallas_call(query_kernel, in_specs=[hbm, hbm, hbm, vmem, hbm, hbm, hbm...  20.4 us

profile of v5, /device:TPU:1, one launch (start us, length us, event | category | flops | bytes accessed | tf_op | source)
XLA Modules:
  0.0 123.0 jit_solution(5577024195508081895)
XLA Ops:
  0.6 101.8 %reduce_all.1 = (bf16[2,2048,640]{2,1,0:T(8,128)(2,1)}, bf16[1024,1280]{1,0:T(8,128)(2,1)}, bf16[4,4,2,2,40,1280]{5,4,3,2,1,0:T(8,128)(2,1)}, bf16[1024,1280]{1,...) custom-call(bf16[1024,1280]{1,0:T(8,128)(2,1)} %k_hbm.1, ...), custom_call_target="tpu_custom_call" | custom-call | tf_op jit(solution)/shard_map/reduce_all/pallas_call | solution.py:562
  102.4 20.4 %queries.1 = (bf16[1024,1280]{1,0:T(8,128)(2,1)}, bf16[2,640,640]{2,1,0:T(8,128)(2,1)}, bf16[2,640,640]{2,1,0:T(8,128)(2,1)}, bf16[2,640,640]{2,1,0:T(8,128)(2,1)}) custom-call(bf16[1024,1280]{1,0:T(8,128)(2,1)} %get-tuple-element.12.normed_hbm, bf16[1024,1280]{1,0:T(8,128)(2,1)} %get-tuple-element.13.q_hbm, bf16[2,2048,640]{2,1,0:T(8,128)(2,1)} %get-tuple-element.14.u_hbm, ...), custom_call_target="tpu_custom_call" | custom-call | tf_op jit(solution)/shard_map/queries/pallas_call | solution.py:674

commit v6 on v5

--- a/solution.py
+++ b/solution.py
@@ -367,7 +367,6 @@
             by_core(t_three, lambda copy: copy.start())
         if step == 4:
             by_core(t_three, lambda copy: copy.wait())
-            t_mate.start()
 
     firsts = []
     for p in range(4):
@@ -464,16 +463,17 @@
     wait_own(2)
     start_all(own_b[1])
     start_all(own_a[0])
-    wait_other(2)
-    start_all(other_b[1])
     wait_own(1)
     start_all(own_b[0])
     start_all(own_fw)
+    wait_other(2)
+    start_all(other_b[1])
     start_all(other_a[0])
     for p in range(4):
         own_a[0][p].wait_recv()
         own_b[0][p].wait_recv()
         late_fw[p].start()
+    t_mate.start()
 
     for copy in q_loads:
         copy.wait()

time: 123 us -> 122 us (level)
    pallas_call x1, Pallas kernels: 102 us -> 101 us  [reduce_all(): pl.pallas_call(reduce_kernel, in_specs=[hbm, hbm, hbm, vmem, hbm, hbm, hb...]
where the time goes in v6:
time: 122 us
  Pallas kernels  121 us (99%)
    pallas_call x1, Pallas kernels, reduce_all(): pl.pallas_call(reduce_kernel, in_specs=[hbm, hbm, hbm, vmem, hbm, hbm, hb...  101 us
    pallas_call x1, Pallas kernels, queries(): pl.pallas_call(query_kernel, in_specs=[hbm, hbm, hbm, vmem, hbm, hbm, hbm...  20.4 us

profile of v6, /device:TPU:1, one launch (start us, length us, event | category | flops | bytes accessed | tf_op | source)
XLA Modules:
  0.0 121.8 jit_solution(12701202956434975271)
XLA Ops:
  0.6 100.6 %reduce_all.1 = (bf16[2,2048,640]{2,1,0:T(8,128)(2,1)}, bf16[1024,1280]{1,0:T(8,128)(2,1)}, bf16[4,4,2,2,40,1280]{5,4,3,2,1,0:T(8,128)(2,1)}, bf16[1024,1280]{1,...) custom-call(bf16[1024,1280]{1,0:T(8,128)(2,1)} %k_hbm.1, ...), custom_call_target="tpu_custom_call" | custom-call | tf_op jit(solution)/shard_map/reduce_all/pallas_call | solution.py:562
  101.2 20.4 %queries.1 = (bf16[1024,1280]{1,0:T(8,128)(2,1)}, bf16[2,640,640]{2,1,0:T(8,128)(2,1)}, bf16[2,640,640]{2,1,0:T(8,128)(2,1)}, bf16[2,640,640]{2,1,0:T(8,128)(2,1)}) custom-call(bf16[1024,1280]{1,0:T(8,128)(2,1)} %get-tuple-element.12.normed_hbm, bf16[1024,1280]{1,0:T(8,128)(2,1)} %get-tuple-element.13.q_hbm, bf16[2,2048,640]{2,1,0:T(8,128)(2,1)} %get-tuple-element.14.u_hbm, ...), custom_call_target="tpu_custom_call" | custom-call | tf_op jit(solution)/shard_map/queries/pallas_call | solution.py:674
